TPU v7x, 256 devices: a whole 4x4x8 slice. The times are simulated.
256 devices in a mesh: wide: 32 (over z, y), narrow: 8 (over x, core).
Axes of the slice: x: 4, y: 4, z: 8, core: 2. Of those that a mesh axis runs over, the one named last changes fastest.
Arguments:
- hidden: bfloat16 [160, 4096], P('wide', 'narrow'), may hold values from -18 to 18
- w_query: bfloat16 [4096, 4096], P('narrow', 'wide'), may hold values from -0.09375 to 0.09375
- w_keyval: bfloat16 [4096, 1024], P('narrow', 'wide'), may hold values from -0.09375 to 0.09375
- w_out: bfloat16 [4096, 4096], P('narrow', 'wide'), may hold values from -0.09375 to 0.09375
- pool: bfloat16 [16384, 16, 1024], P(('wide', 'narrow')), may hold values from -144 to 144
- page_req: int32 [16384], P(('wide', 'narrow')), may hold values from -1 to 31, as said below
- page_idx: int32 [16384], P(('wide', 'narrow')), may hold values from -1 to 511, as said below
- lengths: int32 [32], replicated, may hold values from 128 to 8192, as said below
- moves: int32 [16384, 1], P(('wide', 'narrow')), may hold values from 0 to 31; in each aligned block of 64 rows (0 to 63, 64 to 127, ...) at most 2 rows name the same one
- accepted: int32 [32], replicated, may hold values from 1 to 5
Outputs:
- attended: bfloat16 [160, 4096], P('narrow', 'wide')
- new_entries: bfloat16 [32, 5, 1024], P('wide')
- moved_pool: bfloat16 [16384, 16, 1024], P(('wide', 'narrow'))
- moved_req: int32 [16384], P(('wide', 'narrow'))
- moved_idx: int32 [16384], P(('wide', 'narrow'))
Inputs may be any that keep to these rules, and one draw needn't show every extreme that they name: Request r holds exactly ceil(lengths[r] / 16) slots, whose page numbers are 0 up to that count minus 1, each once; every other slot is free, with page_req and page_idx -1. `page_idx`: see page_req. `lengths`: each length lies either in 128 to 256 or in 6144 to 8192; exactly 16 lie in the second range. `moves`: each device sends exactly 2 of its slots to each index of wide.
All inputs are finite; a program needn't handle non-finite values.
Results may differ from a plain program's by a relative error of at most 0.03.
Values may be sent and summed in bfloat16 or wider, within the bound.
A program may use at most 128 MiB of HBM per device.

v0:
```python
import math

import jax
import jax.numpy as jnp
from jax import lax
from jax.sharding import PartitionSpec as P

HEADS = 32
KVH = 4
HD = 128
STEPS = 5
PAGE = 16


NEG_FILL = -1e30


def combine(first, second):
    peak = jnp.maximum(first[0], second[0])
    lead = jnp.exp(first[0] - peak)
    trail = jnp.exp(second[0] - peak)
    return (
        peak,
        first[1] * lead + second[1] * trail,
        first[2] * lead[..., None] + second[2] * trail[..., None],
    )


def on_device(hidden, w_query, w_keyval, w_out, pool, page_req, page_idx, lengths, moves, accepted):
    wide_count = lax.axis_size("wide")
    narrow_count = lax.axis_size("narrow")
    groups = HEADS // KVH
    scale = 1.0 / math.sqrt(HD)
    rows_all = lax.all_gather(hidden, "wide", axis=0, tiled=True)
    total_rows = rows_all.shape[0]
    req_total = total_rows // STEPS
    joined = jnp.concatenate([w_query, w_keyval], axis=1)
    query_cols = w_query.shape[1]
    picked = rows_all
    projected = lax.psum_scatter(
        jnp.dot(picked, joined, preferred_element_type=jnp.float32),
        "narrow",
        scatter_dimension=0,
        tiled=True,
    ).astype(jnp.bfloat16)
    query_rows, keyval_rows = (
        lax.all_gather(projected[:, :query_cols], "narrow", axis=0, tiled=True),
        lax.all_gather(projected[:, query_cols:], "narrow", axis=0, tiled=True),
    )
    query_full, keyval_full = (
        lax.all_gather(query_rows, "wide", axis=1, tiled=True),
        lax.all_gather(keyval_rows, "wide", axis=1, tiled=True),
    )
    query = query_full.reshape(req_total, STEPS, KVH, groups, HD)
    keyval = keyval_full.reshape(req_total, STEPS, 2, KVH, HD)
    pool_size = pool.shape[0]
    capacity = pool_size // wide_count
    dest = moves[:, 0]
    order = jnp.arange(pool_size, dtype=jnp.int32)
    rank = jnp.sum((dest[:, None] == dest[None, :]) & (order[None, :] < order[:, None]), axis=1)
    target = dest * capacity + rank
    source_of = jnp.sum(jnp.where(target[None, :] == order[:, None], order[None, :], 0), axis=1)
    moved = (
        lax.all_to_all(
            jnp.take(pool, source_of, axis=0), "wide", split_axis=0, concat_axis=0, tiled=True
        ),
        lax.all_to_all(
            jnp.take(page_req, source_of), "wide", split_axis=0, concat_axis=0, tiled=True
        ),
        lax.all_to_all(
            jnp.take(page_idx, source_of), "wide", split_axis=0, concat_axis=0, tiled=True
        ),
    )
    pages = moved[0]
    requests = moved[1]
    count = pages.shape[0]
    owners = jnp.maximum(requests, 0)
    cache = pages.reshape(count, PAGE, 2, KVH, HD)
    page_query = jnp.take(query, owners, axis=0)
    scores = (
        jnp.einsum(
            "pskgd,ptkd->pkgst", page_query, cache[:, :, 0], preferred_element_type=jnp.float32
        )
        * scale
    )
    positions = moved[2][:, None] * PAGE + jnp.arange(PAGE, dtype=jnp.int32)[None, :]
    visible = (positions < jnp.take(lengths, owners)[:, None]) & (requests >= 0)[:, None]
    visible = visible[:, None, None, None, :]
    scores = jnp.where(visible, scores, NEG_FILL)
    peaks = jnp.max(scores, axis=-1)
    weights = jnp.where(visible, jnp.exp(scores - peaks[..., None]), 0.0)
    totals = jnp.sum(weights, axis=-1)
    sums = jnp.einsum(
        "pkgst,ptkd->pkgsd",
        weights.astype(jnp.bfloat16),
        cache[:, :, 1],
        preferred_element_type=jnp.float32,
    )
    member = requests[None, :] == jnp.arange(req_total, dtype=jnp.int32)[:, None]
    req_peaks = jnp.max(jnp.where(member[:, :, None, None, None], peaks[None], NEG_FILL), axis=1)
    factor = jnp.exp(peaks - jnp.take(req_peaks, owners, axis=0))
    selector = member.astype(jnp.float32)
    req_totals = jnp.dot(
        selector, (totals * factor).reshape(count, -1), precision=lax.Precision.HIGHEST
    )
    req_sums = jnp.dot(
        selector, (sums * factor[..., None]).reshape(count, -1), precision=lax.Precision.HIGHEST
    )
    req_totals = req_totals.reshape(req_total, KVH, groups, STEPS)
    req_sums = req_sums.reshape(req_total, KVH, groups, STEPS, HD)
    row_peaks = jnp.transpose(req_peaks, (0, 3, 1, 2)).reshape(total_rows, HEADS)
    row_totals = jnp.transpose(req_totals, (0, 3, 1, 2)).reshape(total_rows, HEADS)
    row_sums = jnp.transpose(req_sums, (0, 3, 1, 2, 4)).reshape(total_rows, HEADS, HD)
    state = (row_peaks, row_totals, row_sums)
    fresh_scores = (
        jnp.einsum("rskgd,rtkd->rkgst", query, keyval[:, :, 0], preferred_element_type=jnp.float32)
        * scale
    )
    causal = jnp.arange(STEPS)[None, :] <= jnp.arange(STEPS)[:, None]
    fresh_scores = jnp.where(causal, fresh_scores, NEG_FILL)
    fresh_peaks = jnp.max(fresh_scores, axis=-1)
    fresh_weights = jnp.where(causal, jnp.exp(fresh_scores - fresh_peaks[..., None]), 0.0)
    fresh_totals = jnp.sum(fresh_weights, axis=-1)
    fresh_sums = jnp.einsum(
        "rkgst,rtkd->rskgd",
        fresh_weights.astype(jnp.bfloat16),
        keyval[:, :, 1],
        preferred_element_type=jnp.float32,
    )
    self_peaks = jnp.transpose(fresh_peaks, (0, 3, 1, 2)).reshape(total_rows, HEADS)
    self_totals = jnp.transpose(fresh_totals, (0, 3, 1, 2)).reshape(total_rows, HEADS)
    self_sums = fresh_sums.reshape(total_rows, HEADS, HD)
    head_count = HEADS // narrow_count
    first_head = lax.axis_index("narrow") * head_count
    mine_peaks = lax.dynamic_slice_in_dim(self_peaks, first_head, head_count, 1)
    mine_totals = lax.dynamic_slice_in_dim(self_totals, first_head, head_count, 1)
    mine_sums = lax.dynamic_slice_in_dim(self_sums, first_head, head_count, 1)
    peak_all = lax.pmax(state[0], ("wide", "narrow"))
    lead = jnp.exp(state[0] - peak_all)
    scaled_sums = (state[2] * lead[..., None]).reshape(total_rows, HEADS * HD)
    part_sums, part_totals = (
        lax.psum_scatter(
            scaled_sums.astype(jnp.bfloat16), "narrow", scatter_dimension=1, tiled=True
        ).astype(jnp.float32),
        lax.psum_scatter(
            (state[1] * lead).astype(jnp.bfloat16), "narrow", scatter_dimension=1, tiled=True
        ).astype(jnp.float32),
    )
    full_sums, full_totals = (
        lax.psum(part_sums.astype(jnp.bfloat16), "wide").astype(jnp.float32),
        lax.psum(part_totals.astype(jnp.bfloat16), "wide").astype(jnp.float32),
    )
    block_peaks = lax.dynamic_slice_in_dim(peak_all, first_head, head_count, 1)
    final = combine(
        (block_peaks, full_totals, full_sums.reshape(total_rows, head_count, HD)),
        (mine_peaks, mine_totals, mine_sums),
    )
    attn_block = (
        (final[2] / final[1][..., None]).reshape(total_rows, head_count * HD).astype(jnp.bfloat16)
    )
    picked = attn_block
    attended = lax.psum_scatter(
        jnp.dot(picked, w_out, preferred_element_type=jnp.float32).astype(jnp.bfloat16),
        "narrow",
        scatter_dimension=0,
        tiled=True,
    )
    local_req = hidden.shape[0] // STEPS
    first_req = lax.axis_index("wide") * local_req
    fresh_rows = lax.dynamic_slice_in_dim(
        keyval_full.reshape(req_total, STEPS, -1), first_req, local_req, 0
    )
    kept = lax.dynamic_slice_in_dim(accepted, first_req, local_req, 0)
    step_ids = jnp.arange(STEPS, dtype=jnp.int32)
    new_entries = jnp.where(
        step_ids[None, :, None] < kept[:, None, None], fresh_rows, jnp.zeros((), jnp.bfloat16)
    )
    return (attended, new_entries, moved[0], moved[1], moved[2])


def solution(mesh):
    in_specs = (
        P("wide", "narrow"),
        P("narrow", "wide"),
        P("narrow", "wide"),
        P("narrow", "wide"),
        P(("wide", "narrow"), None, None),
        P(("wide", "narrow")),
        P(("wide", "narrow")),
        P(),
        P(("wide", "narrow"), None),
        P(),
    )
    out_specs = (
        P("narrow", "wide"),
        P("wide", None, None),
        P(("wide", "narrow"), None, None),
        P(("wide", "narrow")),
        P(("wide", "narrow")),
    )
    return jax.shard_map(
        on_device, mesh=mesh, in_specs=in_specs, out_specs=out_specs, check_vma=False
    )
```

profile of v0, /device:TPU:1, one launch (start us, length us, event | category | flops | bytes accessed | tf_op | source)
XLA Modules:
  0.0 752.2 jit_solution(15309788727797275602)
XLA Ops:
  7.2 1.0 convert_reduce_fusion
  9.0 1.4 gather_fusion.5
  10.4 1.4 gather_fusion.4
  12.6 12.0 %all-to-all-start = ((s32[32,2,1]{1,2,0:T(1,128)}), s32[32,2,1]{1,2,0:T(1,128)S(1)}, u32[]{:S(2)}, u32[]{:S(2)}) async-start(s32[32,2,1]{1,2,0:T(1,128)} %bitcast.1), calls=%async_computation | async-start | bytes 32768 | tf_op jit(solution)/shard_map/all_to_all | solution.py:67
  25.4 2.0 gather_fusion.1
  27.4 5.8 all-to-all-done
  33.1 3.9 all-to-all-start.1
  37.0 3.2 broadcast_select_fusion.1
  40.2 5.4 all-to-all-done.1
  45.6 4.8 all-to-all-start.2
  50.4 77.1 %all-gather = bf16[32,5,512]{2,1,0:T(8,128)(2,1)S(1)} all-gather(bf16[1,5,512]{2,1,0:T(8,128)(2,1)S(1)} %bitcast.133), channel_id=1, replica_groups=mesh['wide'=32,'narrow'=8] {'wide'}, dimensions={0}, use_global_device_ids=true | all-gather | bytes 168960 | tf_op jit(solution)/shard_map/all_gather | solution.py:34
  129.3 34.6 %all-reduce = bf16[160,160]{0,1:T(8,128)(2,1)S(1)} all-reduce(f32[160,160]{0,1:T(8,128)S(1)} %convolution_bitcast_fusion.1), channel_id=2, replica_groups=mesh['wide'=32,'narrow'=8] {'narrow'}, use_global_device_ids=true, to_apply=%region_2.0.clone | all-reduce | flops 25600 | bytes 153600
  164.1 15.9 %all-gather.1 = bf16[8,20,128]{2,1,0:T(8,128)(2,1)S(1)} all-gather(bf16[1,20,128]{2,1,0:T(8,128)(2,1)S(1)} %copy.106), channel_id=1, replica_groups=mesh['wide'=32,'narrow'=8] {'narrow'}, dimensions={0}, use_global_device_ids=true | all-gather | bytes 46080 | tf_op jit(solution)/shard_map/all_gather | solution.py:47
  184.4 62.4 %all-gather.5.cloned.1.call-done = bf16[160,4096]{1,0:T(8,128)(2,1)} async-done(((bf16[160,128]{1,0:T(8,128)(2,1)}), bf16[160,4096]{1,0:T(8,128)(2,1)}) %all-gather.5.cloned.1.call-update) | async-done | bytes 1310736 | tf_op jit(solution)/shard_map/all_gather | solution.py:51
  246.8 1.6 copy.169
  248.4 2.4 gather_fusion.2
  250.8 4.4 reshape.221
  255.2 3.7 fusion.50
  258.9 3.5 bitcast_reduce_fusion
  262.8 1.2 copy.137
  265.7 1.0 gather_fusion.3
  267.9 6.2 fusion.4
  274.1 1.8 copy.136
  277.1 79.0 %pmax.7 = f32[160,32]{0,1:T(8,128)S(1)} all-reduce(f32[160,32]{0,1:T(8,128)S(1)} %copy.119), channel_id=1, replica_groups=mesh['wide'=32,'narrow'=8] {'wide','narrow'}, use_global_device_ids=true, to_apply=%region_5.7 | all-reduce | flops 5120 | bytes 40960 | tf_op jit(solution)/shard_map/pmax | solution.py:138
  356.2 0.9 subtract_exponential_fusion
  357.1 1.8 copy.113
  358.8 5.5 broadcast_multiply_fusion
  364.3 5.1 copy.114
  369.4 6.7 reshape.223
  376.2 7.3 dot_general.39
  383.5 8.2 %fusion.17 = f32[32,5,4,8,128]{4,0,1,3,2:T(8,128)S(1)} fusion(f32[4,8,5,128,64]{3,2,1,0,4:T(8,128)} %dot_general.39, s32[64]{0:T(128)S(1)} %eq.48), kind=kOutput, calls=%fused_computation.30 | convolution fusion | flops 503318528 | bytes 7864576 | tf_op jit(solution)/shard_map/dot_general | solution.py:106
  391.7 3.0 copy.116
  394.7 4.0 reshape.224
  399.4 1.0 copy-done.3
  400.4 2.6 fusion.8
  403.9 13.3 %all-gather.2 = bf16[8,20,32]{2,1,0:T(8,128)(2,1)S(1)} all-gather(bf16[1,20,32]{2,1,0:T(8,128)(2,1)S(1)} %copy.121), channel_id=1, replica_groups=mesh['wide'=32,'narrow'=8] {'narrow'}, dimensions={0}, use_global_device_ids=true | all-gather | bytes 11520 | tf_op jit(solution)/shard_map/all_gather | solution.py:48
  417.3 38.1 %all_gather.19 = bf16[160,1024]{0,1:T(8,128)(2,1)S(1)} all-gather(bf16[160,32]{0,1:T(8,128)(2,1)S(1)} %copy.155), channel_id=1, replica_groups=mesh['wide'=32,'narrow'=8] {'wide'}, dimensions={1}, use_global_device_ids=true | all-gather | bytes 337920 | tf_op jit(solution)/shard_map/all_gather | solution.py:52
  458.6 6.4 fusion.20
  465.0 2.5 copy.126
  468.8 2.3 copy.133
  472.0 1.8 copy.134
  473.9 31.5 %all-reduce.1 = bf16[160,32]{1,0:T(8,128)(2,1)S(1)} all-reduce(bf16[160,32]{1,0:T(8,128)(2,1)S(1)} %copy.142), channel_id=4, replica_groups=mesh['wide'=32,'narrow'=8] {'narrow'}, use_global_device_ids=true, to_apply=%region_10.12.clone | all-reduce | flops 5120 | bytes 20480
  505.5 58.2 %psum.15 = bf16[160,4]{0,1:T(4,128)(2,1)S(1)} all-reduce(bf16[160,4]{0,1:T(4,128)(2,1)S(1)} %copy.143), channel_id=1, replica_groups=mesh['wide'=32,'narrow'=8] {'wide'}, use_global_device_ids=true, to_apply=%region_11.13 | all-reduce | flops 640 | bytes 2560 | tf_op jit(solution)/shard_map/psum | solution.py:151
  563.7 1.6 reshape.226
  565.8 147.4 %all-reduce.5.cloned.1.call-done = bf16[160,4,128]{2,1,0:T(4,128)(2,1)} async-done(((bf16[160,4,128]{2,1,0:T(4,128)(2,1)}), bf16[160,4,128]{2,1,0:T(4,128)(2,1)}) %all-reduce.5.cloned.1.call-update) | async-done | bytes 163856 | tf_op jit(solution)/shard_map/psum | solution.py:150
  713.2 1.8 fusion.25
  715.2 26.3 %all-reduce.2 = bf16[160,128]{1,0:T(8,128)(2,1)S(1)} all-reduce(bf16[160,128]{1,0:T(8,128)(2,1)S(1)} %convolution_convert_fusion), channel_id=5, replica_groups=mesh['wide'=32,'narrow'=8] {'narrow'}, use_global_device_ids=true, to_apply=%region_13.15.clone | all-reduce | flops 20480 | bytes 81920
  742.2 3.2 copy.201
  (126 shorter events, 20.1 us)
Async XLA Ops:
  7.2 18.2 %copy-start = (bf16[64,16,1024]{2,1,0:T(8,128)(2,1)S(1)}, bf16[64,16,1024]{2,1,0:T(8,128)(2,1)}, u32[]{:S(2)}) copy-start(bf16[64,16,1024]{2,1,0:T(8,128)(2,1)} %param.16) | copy-start | bytes 6291460
  12.6 20.6 %all-to-all-start = ((s32[32,2,1]{1,2,0:T(1,128)}), s32[32,2,1]{1,2,0:T(1,128)S(1)}, u32[]{:S(2)}, u32[]{:S(2)}) async-start(s32[32,2,1]{1,2,0:T(1,128)} %bitcast.1), calls=%async_computation | async-start | bytes 32768 | tf_op jit(solution)/shard_map/all_to_all | solution.py:67
  33.1 12.4 %all-to-all-start.1 = ((s32[32,2,1]{1,2,0:T(1,128)}), s32[32,2,1]{1,2,0:T(1,128)S(1)}, u32[]{:S(2)}, u32[]{:S(2)}) async-start(s32[32,2,1]{1,2,0:T(1,128)} %bitcast.4), calls=%async_computation.1 | async-start | bytes 32768 | tf_op jit(solution)/shard_map/all_to_all | solution.py:70
  40.2 10.3 %copy-start.12 = (bf16[5,512]{1,0:T(8,128)(2,1)S(1)}, bf16[5,512]{1,0:T(8,128)(2,1)}, u32[]{:S(2)}) copy-start(bf16[5,512]{1,0:T(8,128)(2,1)} %param.12) | copy-start | bytes 15364
  40.2 87.5 %copy-start.10 = (bf16[512,32]{0,1:T(8,128)(2,1)S(1)}, bf16[512,32]{0,1:T(8,128)(2,1)}, u32[]{:S(2)}) copy-start(bf16[512,32]{0,1:T(8,128)(2,1)} %param.14) | copy-start | bytes 98308
  40.2 87.6 %copy-start.18 = (u32[256]{0:T(256)S(1)}, u32[256]{0:T(256)}, u32[]{:S(2)}) copy-start(u32[256]{0:T(256)} %constant.105) | copy-start | bytes 3076
  40.2 88.9 %copy-start.16 = (bf16[512,128]{1,0:T(8,128)(2,1)S(1)}, bf16[512,128]{1,0:T(8,128)(2,1)}, u32[]{:S(2)}) copy-start(bf16[512,128]{1,0:T(8,128)(2,1)} %param.13) | copy-start | bytes 393220
  40.2 143.3 %copy-start.2 = (s32[32]{0:T(128)S(1)}, s32[32]{0:T(128)}, u32[]{:S(2)}) copy-start(s32[32]{0:T(128)} %param.19) | copy-start | bytes 388
  45.6 205.2 %all-to-all-start.2 = ((bf16[64,16,1024]{2,1,0:T(8,128)(2,1)}), bf16[64,16,1024]{2,1,0:T(8,128)(2,1)}, u32[]{:S(2)}, u32[]{:S(2)}) async-start(bf16[64,16,1024]{2,1,0:T(8,128)(2,1)} %broadcast_select_fusion.1), calls=%async_computation.2 | async-start | bytes 4194304 | tf_op jit(solution)/shard_map/all_to_all | solution.py:64
  50.4 196.4 %all-gather.5.cloned.1.call-start = ((), (), s32[]{:S(2)}) async-start(), calls=%async_computation.4 | async-start | bytes 1351680 | tf_op jit(solution)/shard_map/all_gather | solution.py:51
  164.0 82.8 %copy-start.8 = (bf16[20,160]{0,1:T(8,128)(2,1)}, bf16[20,160]{0,1:T(8,128)(2,1)S(1)}, u32[]{:S(2)}) copy-start(bf16[20,160]{0,1:T(8,128)(2,1)S(1)} %dynamic-slice_convert_fusion) | copy-start | bytes 19204
  180.6 383.1 %reduce-scatter.4.cloned.1.call-start = ((), (), s32[]{:S(2)}) async-start(), calls=%async_computation.5 | async-start | bytes 1474560 | tf_op jit(solution)/shard_map/reduce_scatter | solution.py:142
  182.5 201.0 %copy-start.11 = (s32[64]{0:T(128)}, s32[64]{0:T(128)S(1)}, u32[]{:S(2)}) copy-start(s32[64]{0:T(128)S(1)} %eq.48) | copy-start | bytes 772
  183.4 67.3 %copy-start.15 = (s32[64]{0:T(128)}, s32[64]{0:T(128)S(1)}, u32[]{:S(2)}) copy-start(s32[64]{0:T(128)S(1)} %all_to_all.21) | copy-start | bytes 772
  184.3 91.8 %copy-start.13 = (pred[64]{0:T(512)(128)(4,1)}, pred[64]{0:T(512)(128)(4,1)S(1)}, u32[]{:S(2)}) copy-start(pred[64]{0:T(512)(128)(4,1)S(1)} %get-tuple-element.22) | copy-start | bytes 196
  255.2 3.7 copy-start.6
  264.8 0.8 copy-start.4
  267.9 8.0 %copy-start.7 = (f32[64,4,8,5]{0,3,2,1:T(8,128)S(1)}, f32[64,4,8,5]{0,3,2,1:T(8,128)}, u32[]{:S(2)}) copy-start(f32[64,4,8,5]{0,3,2,1:T(8,128)} %copy.137) | copy-start | bytes 122884
  274.1 2.6 copy-start.5
  276.0 80.1 %copy-start.14 = (pred[64]{0:T(512)(128)(4,1)S(1)}, pred[64]{0:T(512)(128)(4,1)}, u32[]{:S(2)}) copy-start(pred[64]{0:T(512)(128)(4,1)} %copy-done.13) | copy-start | bytes 196
  398.7 1.7 copy-start.3
  403.0 53.5 %copy-start.17 = (s32[32]{0:T(128)S(1)}, s32[32]{0:T(128)}, u32[]{:S(2)}) copy-start(s32[32]{0:T(128)} %param.21) | copy-start | bytes 388
  403.0 310.1 %all-reduce.5.cloned.1.call-start = ((), (), s32[]{:S(2)}) async-start(), calls=%async_computation.6 | async-start | bytes 327680 | tf_op jit(solution)/shard_map/psum | solution.py:150
  471.9 243.1 %copy-start.9 = (bf16[512,128]{1,0:T(8,128)(2,1)S(1)}, bf16[512,128]{1,0:T(8,128)(2,1)}, u32[]{:S(2)}) copy-start(bf16[512,128]{1,0:T(8,128)(2,1)} %param.15) | copy-start | bytes 393220
  713.2 32.2 %copy-start.1 = (bf16[64,16,1024]{2,1,0:T(8,128)(2,1)S(1)}, bf16[64,16,1024]{2,1,0:T(8,128)(2,1)}, u32[]{:S(2)}) copy-start(bf16[64,16,1024]{2,1,0:T(8,128)(2,1)} %param.16) | copy-start | bytes 6291460
Sparse Core Ops, SparseCore 0:
  180.8 65.9 all-gather.4
  403.2 28.0 reduce-scatter.3
  565.5 147.6 all-reduce.4
where the time goes:
time: 758 us; the launch traced here: 752 us
  blocking collectives  374 us (49%)
  waiting for transfers between devices  221 us (29%)
  local copies, waits for them, and re-layouts  74.7 us (10%)
  matrix products  24.9 us (3%)
  starting transfers between devices  21.2 us (3%)
  other arithmetic  20.5 us (3%)
  between operations  15.9 us (2%)
    psum x1, waiting for transfers between devices, on_device(): lax.psum(part_sums.astype(jnp.bfloat16), 'wide').astype(jnp.float32)  147 us
    unnamed x3, blocking collectives  92.4 us
    pmax x1, blocking collectives, on_device(): peak_all = lax.pmax(state[0], ('wide', 'narrow'))  79 us
    all_gather x1, blocking collectives, on_device(): rows_all = lax.all_gather(hidden, 'wide', axis=0, tiled=True)  77.1 us
    all_gather x1, waiting for transfers between devices, on_device(): lax.all_gather(query_rows, 'wide', axis=1, tiled=True)  62.4 us
    psum x1, blocking collectives, on_device(): lax.psum(part_totals.astype(jnp.bfloat16), 'wide').astype(jnp.float32)  58.2 us
    all_gather x1, blocking collectives, on_device(): lax.all_gather(keyval_rows, 'wide', axis=1, tiled=True)  38.1 us
    all_gather x1, blocking collectives, on_device(): lax.all_gather(projected[:, :query_cols], 'narrow', axis=0, tiled=True)  15.9 us
  transfers between devices with their start and end apart: 6, of which 4 were waited for; matrix products, arithmetic and copies ran while one was open for 4% of the time, Pallas kernels for 0%

commit v1 on v0

v1 whole, which is shorter than its diff:
```python
import functools
import math

import jax
import jax.numpy as jnp
from jax import lax
from jax.experimental import pallas as pl
from jax.experimental.pallas import tpu as pltpu
from jax.sharding import PartitionSpec as P

HEADS = 32
KVH = 4
HD = 128
STEPS = 5
PAGE = 16
WIDE = 32
NARROW = 8
NY = 4
NZ = 8
POOL = 64
CHUNK = 16
SCALE = 1.0 / math.sqrt(HD)
LOG2E = 1.4426950408889634
NEG = -1e30
F32 = jnp.float32
BF16 = jnp.bfloat16
I32 = jnp.int32
MESH = pl.DeviceIdType.MESH
VMEM_SPEC = pl.BlockSpec(memory_space=pltpu.VMEM)
SMEM_SPEC = pl.BlockSpec(memory_space=pltpu.SMEM)
ANY_SPEC = pl.BlockSpec(memory_space=pl.ANY)


def sort_kernel(moves, req, idx, lens, pool, sorted_out, live_out, meta, count, sem):
    def clear(d, _):
        count[d] = 0
        return 0

    lax.fori_loop(0, WIDE, clear, 0)

    def place(p, state):
        live, free = state
        d = moves[p]
        k = count[d]
        count[d] = k + 1
        r = req[p]
        i = idx[p]
        pltpu.make_async_copy(pool.at[p], sorted_out.at[k, d], sem.at[0]).start()
        meta[0, 2 * d + k] = r
        meta[0, POOL + 2 * d + k] = i
        alive = r >= 0
        pos = jnp.where(alive, live, POOL - 1 - free)
        pltpu.make_async_copy(pool.at[p], live_out.at[pos], sem.at[1]).start()
        seen = jnp.clip(lens[jnp.maximum(r, 0)] - i * PAGE, 0, PAGE)
        meta[1, pos] = r
        meta[1, POOL + pos] = jnp.where(alive, seen, 0)
        step = jnp.where(alive, 1, 0)
        return live + step, free + 1 - step

    live, _ = lax.fori_loop(0, POOL, place, (jnp.int32(0), jnp.int32(0)))
    meta[2, 0] = live
    pltpu.make_async_copy(live_out, live_out, sem.at[0]).wait()
    pltpu.make_async_copy(live_out, live_out, sem.at[1]).wait()


def enter(w, n):
    barrier = pltpu.get_barrier_semaphore()

    def wide_signal(k, _):
        pl.semaphore_signal(
            barrier, inc=1, device_id=((w + k) % WIDE, n), device_id_type=MESH
        )
        return 0

    def narrow_signal(k, _):
        pl.semaphore_signal(
            barrier, inc=1, device_id=(w, (n + k) % NARROW), device_id_type=MESH
        )
        return 0

    lax.fori_loop(1, WIDE, wide_signal, 0)
    lax.fori_loop(1, NARROW, narrow_signal, 0)
    pl.semaphore_wait(barrier, WIDE + NARROW - 2)


def remote(src, dst, send, recv, device):
    return pltpu.make_async_remote_copy(
        src_ref=src,
        dst_ref=dst,
        send_sem=send,
        recv_sem=recv,
        device_id=device,
        device_id_type=MESH,
    )


def gather_kernel(
    hidden, w_query, w_kv_t, meta, leaving, pages,
    query_out, kvrow_out, kv_out, moved_out, meta_wide, meta_narrow,
    hid_own, hid_all, send_b, recv_b, q_own, kv_tiles, kv_parts, meta_w, meta_n,
    s_a, r_a, s_m, r_m, s_mn, r_mn, s_mig, r_mig, l_sem, s_x, r_x, s_p, r_p,
    s_b, r_b, s_c1, r_c1, s_k1, r_k1, s_c2, r_c2, s_k2, r_k2, s_c3, r_c3,
):
    w = lax.axis_index("wide")
    n = lax.axis_index("narrow")
    z = w // NY
    y = w % NY
    x = n // 2
    c = n % 2
    other = 2 * x + (1 - c)
    hub = n == z
    hid_own[...] = jnp.zeros_like(hid_own)
    hid_own[0:STEPS, :] = hidden[...]
    hid_all[pl.ds(w, 1)] = hid_own[...][None]
    meta_w[pl.ds(w, 1)] = meta[...][None]
    meta_n[pl.ds(n, 1)] = meta[...][None]
    enter(w, n)

    def send_hidden(k, _):
        remote(hid_own, hid_all.at[w], s_a, r_a, ((w + k) % WIDE, n)).start()
        return 0

    lax.fori_loop(1, WIDE, send_hidden, 0)

    def key_block(head):
        return pl.ds(pl.multiple_of(HD * head, HD), HD)

    def value_block(head):
        return pl.ds(pl.multiple_of(KVH * HD + HD * head, HD), HD)

    for dx in (1, 3, 2):
        tx = (x + dx) % 4
        for part, block in ((0, key_block(tx)), (1, value_block(tx))):
            remote(
                pages.at[:, :, block], kv_out.at[n, part], s_x, r_x.at[dx - 1], (w, 2 * tx + c)
            ).start()
    own_copies = []
    for part, block in ((0, key_block(x)), (1, value_block(x))):
        remote(pages.at[:, :, block], kv_out.at[n, part], s_p, r_p.at[0], (w, other)).start()
        own = pltpu.make_async_copy(pages.at[:, :, block], kv_out.at[n, part], l_sem.at[part])
        own.start()
        own_copies.append(own)

    def send_page(k, _):
        peer = (w + k) % WIDE
        remote(leaving.at[0, peer], moved_out.at[w], s_mig, r_mig, (peer, n)).start()
        return 0

    lax.fori_loop(1, WIDE, send_page, 0)
    stay = pltpu.make_async_copy(leaving.at[0, w], moved_out.at[w], l_sem.at[2])
    stay.start()

    def send_meta(k, _):
        remote(meta, meta_w.at[w], s_m, r_m, ((w + k) % WIDE, n)).start()
        return 0

    def send_meta_narrow(k, _):
        remote(meta, meta_n.at[n], s_mn, r_mn, (w, (n + k) % NARROW)).start()
        return 0

    lax.fori_loop(1, WIDE, send_meta, 0)
    lax.fori_loop(1, NARROW, send_meta_narrow, 0)

    others = hid_all.at[pl.ds(0, WIDE - 1)]
    all_hidden = remote(others, others, s_a, r_a, (w, n))
    all_hidden.wait_recv()
    rows = hid_all[...].reshape(WIDE * 8, hid_all.shape[2])
    part_q = jnp.dot(rows, w_query[...], preferred_element_type=F32)
    part_kv = lax.dot_general(
        rows, w_kv_t[...], (((1,), (1,)), ((), ())), preferred_element_type=F32
    )
    send_b[:, 0:32, :] = part_q.reshape(NARROW, 32, HD)
    part_kv = part_kv.reshape(NARROW, 4, 8, 32)
    for j in range(4):
        send_b[:, 32:40, 32 * j : 32 * j + 32] = part_kv[:, j]
    recv_b[pl.ds(n, 1)] = send_b[pl.ds(n, 1)]

    def send_sums(k, _):
        peer = (n + k) % NARROW
        remote(send_b.at[peer], recv_b.at[n], s_b, r_b, (w, peer)).start()
        return 0

    lax.fori_loop(1, NARROW, send_sums, 0)
    others = recv_b.at[pl.ds(0, NARROW - 1)]
    all_sums = remote(others, others, s_b, r_b, (w, n))
    all_sums.wait_recv()
    total = jnp.sum(recv_b[...], axis=0)
    q_own[...] = total[0:32].astype(BF16)
    kv_sum = total[32:40]
    for j in range(4):
        shifted = pltpu.roll(kv_sum, (y - j + 4) % 4 * 32, 1)
        kv_tiles[j] = shifted.astype(BF16)
    rows_here = pl.ds(pl.multiple_of(32 * n, 32), 32)
    one_query = remote(q_own, query_out.at[y, rows_here], s_c1, r_c1, (w, z))

    @pl.when(n != z)
    def _():
        one_query.start()

    @pl.when(hub)
    def _():
        query_out[pl.ds(y, 1), rows_here] = q_own[...][None]

    for j in range(4):
        target = NY * n + j

        @pl.when(target != w)
        def _():
            remote(kv_tiles.at[j], kv_parts.at[w], s_k1, r_k1, (target, n)).start()

        @pl.when(target == w)
        def _():
            kv_parts[pl.ds(w, 1)] = kv_tiles[j][None]

    mine = query_out.at[y]
    seven = query_out.at[y, pl.ds(0, 224)]
    parts31 = kv_parts.at[pl.ds(0, WIDE - 1)]

    @pl.when(hub)
    def _():
        remote(seven, seven, s_c1, r_c1, (w, n)).wait_recv()

        def send_query(k, _):
            peer = ((z + k) % NZ) * NY + y
            remote(mine, mine, s_c2, r_c2, (peer, n)).start()
            return 0

        lax.fori_loop(1, NZ, send_query, 0)

    @pl.when(n != z)
    def _():
        remote(mine, mine, s_c2, r_c2, (w, n)).wait_recv()

    for dy in (1, 3, 2):
        remote(mine, mine, s_c3, r_c3, (z * NY + (y + dy) % NY, n)).start()

    @pl.when(hub)
    def _():
        remote(parts31, parts31, s_k1, r_k1, (w, n)).wait_recv()
        lane = lax.broadcasted_iota(I32, (8, HD), 1)
        for b in range(8):
            merged = jnp.zeros((8, HD), F32)
            for t in range(4):
                piece = kv_parts[4 * b + t].astype(F32)
                merged = merged + jnp.where((lane >= 32 * t) & (lane < 32 * t + 32), piece, 0.0)
            kvrow_out[:, HD * b : HD * b + HD] = merged.astype(BF16)

        def send_row(k, _):
            remote(kvrow_out, kvrow_out, s_k2, r_k2, (w, (n + k) % NARROW)).start()
            return 0

        lax.fori_loop(1, NARROW, send_row, 0)

    for dx in (1, 3, 2):
        source = 2 * ((x + 4 - dx) % 4) + c
        arrived = kv_out.at[source]
        remote(arrived, arrived, s_x, r_x.at[dx - 1], (w, n)).wait_recv()
        remote(arrived, arrived, s_p, r_p.at[dx], (w, other)).start()

    @pl.when(n != z)
    def _():
        remote(kvrow_out, kvrow_out, s_k2, r_k2, (w, n)).wait_recv()

    wide_tiles = meta_w.at[pl.ds(0, WIDE - 1)]
    narrow_tiles = meta_n.at[pl.ds(0, NARROW - 1)]
    remote(wide_tiles, wide_tiles, s_m, r_m, (w, n)).wait()
    remote(narrow_tiles, narrow_tiles, s_mn, r_mn, (w, n)).wait()
    meta_wide[...] = meta_w[:, 0, :]
    meta_narrow[...] = meta_n[...]
    three = query_out.at[pl.ds(0, 3)]
    remote(three, three, s_c3, r_c3, (w, n)).wait()
    for own in own_copies:
        own.wait()
    stay.wait()
    one = kv_out.at[0]
    for i in range(4):
        remote(one, one, s_p, r_p.at[i], (w, n)).wait_recv()
    three = kv_out.at[pl.ds(0, 3)]
    remote(three, three, s_x, r_x.at[0], (w, n)).wait_send()
    four = kv_out.at[pl.ds(0, 4)]
    remote(four, four, s_p, r_p.at[0], (w, n)).wait_send()
    all_hidden.wait_send()
    all_sums.wait_send()

    @pl.when(n != z)
    def _():
        one_query.wait_send()

    three = kv_tiles.at[pl.ds(0, 3)]
    four = kv_tiles.at[pl.ds(0, 4)]

    @pl.when(hub)
    def _():
        remote(three, three, s_k1, r_k1, (w, n)).wait_send()
        seven_rows = kv_parts.at[pl.ds(0, 28)]
        row7 = query_out.at[pl.ds(0, 3)]
        row4 = query_out.at[pl.ds(0, 4)]
        remote(row7, row7, s_c2, r_c2, (w, n)).wait_send()
        remote(row4, row4, s_c2, r_c2, (w, n)).wait_send()
        for _ in range(7):
            remote(kvrow_out, kvrow_out, s_k2, r_k2, (w, n)).wait_send()

    @pl.when(n != z)
    def _():
        remote(four, four, s_k1, r_k1, (w, n)).wait_send()

    gone = moved_out.at[pl.ds(0, WIDE - 1)]
    remote(gone, gone, s_mig, r_mig, (w, n)).wait()


def payload_stats(peak, total, group, step):
    stat = jnp.where(group == step, peak, jnp.where(group - 8 == step, total, 0.0))
    first = stat.astype(BF16)
    rest = stat - first.astype(F32)
    second = rest.astype(BF16)
    third = (rest - second.astype(F32)).astype(BF16)
    return first, second, third


def attention_kernel(
    counts, meta_rows, accepted, meta_narrow, query, kvrow, kv,
    out, entries, moved_req, moved_idx,
    q_rows, token_req, scores, peaks, acc,
):
    w = lax.axis_index("wide")
    n = lax.axis_index("narrow")
    x = n // 2
    rows = WIDE * STEPS

    def moved_meta(i, _):
        for k in range(2):
            moved_req[2 * i + k] = meta_rows[i, 2 * w + k]
            moved_idx[2 * i + k] = meta_rows[i, POOL + 2 * w + k]
        return 0

    lax.fori_loop(0, WIDE, moved_meta, 0)
    step = lax.broadcasted_iota(I32, (STEPS, KVH * HD * 2), 0)
    entries[0] = jnp.where(
        step < accepted[w], kvrow[0:STEPS, :].astype(F32), 0.0
    ).astype(BF16)

    row = lax.broadcasted_iota(I32, (rows, WIDE * 8), 0).astype(F32)
    col = lax.broadcasted_iota(I32, (rows, WIDE * 8), 1).astype(F32)
    req_of_row = jnp.floor((row + 0.5) * 0.2)
    pick = (col == req_of_row * 3.0 + row).astype(F32).astype(BF16)
    for h in range(4):
        q_rows[rows * h : rows * h + rows, :] = jnp.dot(
            pick, query[h], preferred_element_type=F32
        ).astype(BF16)

    page_meta = meta_narrow[:, 1, :].astype(F32).astype(BF16)
    page = lax.broadcasted_iota(I32, (2 * POOL, POOL * PAGE), 0)
    token = lax.broadcasted_iota(I32, (2 * POOL, POOL * PAGE), 1)
    page_of = token >> 4
    spread_req = (page == page_of).astype(F32).astype(BF16)
    spread_seen = (page - POOL == page_of).astype(F32).astype(BF16)
    owner = jnp.dot(page_meta, spread_req, preferred_element_type=F32)
    seen = jnp.dot(page_meta, spread_seen, preferred_element_type=F32)
    within = (lax.broadcasted_iota(I32, (NARROW, POOL * PAGE), 1) & 15).astype(F32)
    owner = jnp.where(within < seen, owner, -1.0)
    width = CHUNK * PAGE
    per = POOL // CHUNK
    for s in range(NARROW):
        for i in range(per):
            token_req[per * s + i] = jnp.broadcast_to(
                owner[s : s + 1, width * i : width * i + width], (8, width)
            )

    peaks[...] = jnp.full(peaks.shape, NEG, F32)
    acc[...] = jnp.zeros_like(acc)
    all_row = lax.broadcasted_iota(I32, (rows, 1), 0).astype(F32)
    row_req = jnp.floor((all_row + 0.5) * 0.2)
    row_req = jnp.concatenate([row_req] * 4, axis=0)

    base = jnp.int32(0)
    bases = []
    for s in range(NARROW):
        bases.append(base)
        chunks = (counts[s, 0] + (CHUNK - 1)) // CHUNK

        def score(i, _, s=s, base=base):
            keys = kv[s, 0, pl.ds(i * CHUNK, CHUNK)].reshape(width, HD)
            raw = lax.dot_general(
                q_rows[...], keys, (((1,), (1,)), ((), ())), preferred_element_type=F32
            )
            owners = token_req[per * s + i][0:1, :]
            raw = jnp.where(row_req == owners, raw, NEG)
            scores[base + i] = raw
            peaks[...] = jnp.maximum(
                peaks[...], jnp.maximum(raw[:, 0:HD], raw[:, HD : 2 * HD])
            )
            return 0

        lax.fori_loop(0, chunks, score, 0)
        base = base + chunks

    peak = jnp.max(peaks[...], axis=1, keepdims=True)
    ones = jnp.ones((width, HD), BF16)
    for s in range(NARROW):
        chunks = (counts[s, 0] + (CHUNK - 1)) // CHUNK

        def weigh(i, _, s=s, base=bases[s]):
            values = kv[s, 1, pl.ds(i * CHUNK, CHUNK)].reshape(width, HD)
            weights = jnp.exp2((scores[base + i] - peak) * (SCALE * LOG2E)).astype(BF16)
            acc[...] += jnp.dot(
                weights, jnp.concatenate([values, ones], axis=1), preferred_element_type=F32
            )
            return 0

        lax.fori_loop(0, chunks, weigh, 0)

    slot = lax.broadcasted_iota(I32, (WIDE * 8, rows), 0)
    req_of_slot = (slot >> 3).astype(F32)
    place = (slot & 7).astype(F32)
    source = lax.broadcasted_iota(I32, (WIDE * 8, rows), 1).astype(F32)
    req_of_source = jnp.floor((source + 0.5) * 0.2)
    step_of_source = source - req_of_source * 5.0
    same = req_of_slot == req_of_source
    spread = [(same & (place == step_of_source)).astype(F32).astype(BF16)]
    for k in range(3):
        spread.append((same & (place == 5.0 + k)).astype(F32).astype(BF16))
    spread = jnp.concatenate(spread, axis=1)
    group = (lax.broadcasted_iota(I32, (rows, HD), 1) >> 3).astype(F32)
    srow = lax.broadcasted_iota(I32, (rows, HD), 0).astype(F32)
    step_of = srow - jnp.floor((srow + 0.5) * 0.2) * 5.0
    for h in range(4):
        here = slice(rows * h, rows * h + rows)
        terms = payload_stats(peak[here] * SCALE, acc[here, HD:], group, step_of)
        stacked = jnp.concatenate([acc[here, 0:HD].astype(BF16), *terms], axis=0)
        laid = jnp.dot(spread, stacked, preferred_element_type=F32)
        out[0:WIDE, h] = laid.astype(BF16).reshape(WIDE, 8, HD)

    q_new = query[:, pl.ds(pl.multiple_of(8 * w, 8), 8), :].reshape(32, HD)
    k_new = kvrow[:, pl.ds(pl.multiple_of(HD * x, HD), HD)]
    v_new = kvrow[:, pl.ds(pl.multiple_of(KVH * HD + HD * x, HD), HD)]
    fresh = lax.dot_general(
        q_new, k_new, (((1,), (1,)), ((), ())), preferred_element_type=F32
    ) * SCALE
    fresh_row = lax.broadcasted_iota(I32, (32, 8), 0) & 7
    fresh_key = lax.broadcasted_iota(I32, (32, 8), 1)
    known = fresh_key <= fresh_row
    fresh = jnp.where(known, fresh, NEG)
    fresh_peak = jnp.max(fresh, axis=1, keepdims=True)
    fresh_weight = jnp.where(known, jnp.exp(fresh - fresh_peak), 0.0)
    fresh_total = jnp.sum(fresh_weight, axis=1, keepdims=True)
    fresh_sum = jnp.dot(fresh_weight.astype(BF16), v_new, preferred_element_type=F32)
    lane_group = lax.broadcasted_iota(I32, (8, HD), 1) >> 3
    sub = lax.broadcasted_iota(I32, (8, HD), 0)
    for h in range(4):
        here = slice(8 * h, 8 * h + 8)
        stat = jnp.where(
            lane_group == sub,
            fresh_peak[here],
            jnp.where(lane_group - 8 == sub, fresh_total[here], 0.0),
        )
        line = jnp.sum(jnp.where(sub < STEPS, stat, 0.0), axis=0, keepdims=True)
        first = line.astype(BF16).astype(F32)
        second = (line - first).astype(BF16).astype(F32)
        third = line - first - second
        tile = jnp.where(
            sub < STEPS,
            fresh_sum[here],
            jnp.where(sub == 5, first, jnp.where(sub == 6, second, third)),
        )
        out[WIDE, h] = tile.astype(BF16)


def combine_kernel(
    partial, w_out, leaving,
    attended, moved_out,
    received, own, gathered, send_e, recv_e,
    s_d, r_d, s_g, r_g, s_e, r_e, s_mig, r_mig, l_sem,
):
    w = lax.axis_index("wide")
    n = lax.axis_index("narrow")
    received[pl.ds(w, 1)] = partial[pl.ds(w, 1)]
    received[WIDE] = partial[WIDE]
    enter(w, n)

    def send_partial(k, _):
        peer = (w + k) % WIDE
        remote(partial.at[peer], received.at[w], s_d, r_d, (peer, n)).start()
        return 0

    lax.fori_loop(1, WIDE, send_partial, 0)

    def send_page(k, _):
        peer = (w + k) % WIDE
        remote(leaving.at[1, peer], moved_out.at[w], s_mig, r_mig, (peer, n)).start()
        return 0

    lax.fori_loop(1, WIDE, send_page, 0)
    stay = pltpu.make_async_copy(leaving.at[1, w], moved_out.at[w], l_sem)
    stay.start()
    others = received.at[pl.ds(0, WIDE - 1)]
    all_partial = remote(others, others, s_d, r_d, (w, n))
    all_partial.wait_recv()
    sub = lax.broadcasted_iota(I32, (1, 8, HD), 1)
    group = lax.broadcasted_iota(I32, (1, 8, HD), 2) >> 3
    for h in range(4):
        tiles = received[:, h].astype(F32)
        line = (tiles[:, 7:8] + tiles[:, 6:7]) + tiles[:, 5:6]
        peak = jnp.max(jnp.where(group == sub, line, -3e38), axis=2, keepdims=True)
        total = jnp.max(jnp.where(group - 8 == sub, line, 0.0), axis=2, keepdims=True)
        top = jnp.max(peak, axis=0, keepdims=True)
        factor = jnp.exp(peak - top)
        total = jnp.sum(factor * total, axis=0)
        sums = jnp.sum(factor * tiles, axis=0)
        own[:, HD * h : HD * h + HD] = jnp.where(
            sub[0] < STEPS, sums / jnp.where(sub[0] < STEPS, total, 1.0), 0.0
        ).astype(BF16)
    gathered[pl.ds(w, 1)] = own[...][None]

    def send_own(k, _):
        remote(own, gathered.at[w], s_g, r_g, ((w + k) % WIDE, n)).start()
        return 0

    lax.fori_loop(1, WIDE, send_own, 0)
    others = gathered.at[pl.ds(0, WIDE - 1)]
    all_rows = remote(others, others, s_g, r_g, (w, n))
    all_rows.wait_recv()
    rows = gathered[...].reshape(WIDE * 8, gathered.shape[2])
    product = jnp.dot(rows, w_out[...], preferred_element_type=F32)
    send_e[...] = product.astype(BF16).reshape(NARROW, 32, HD)
    recv_e[pl.ds(n, 1)] = send_e[pl.ds(n, 1)]

    def send_product(k, _):
        peer = (n + k) % NARROW
        remote(send_e.at[peer], recv_e.at[n], s_e, r_e, (w, peer)).start()
        return 0

    lax.fori_loop(1, NARROW, send_product, 0)
    others = recv_e.at[pl.ds(0, NARROW - 1)]
    all_products = remote(others, others, s_e, r_e, (w, n))
    all_products.wait_recv()
    total = jnp.sum(recv_e[...].astype(F32), axis=0)
    for j in range(4):
        attended[STEPS * j : STEPS * j + STEPS, :] = total[8 * j : 8 * j + STEPS].astype(BF16)
    all_partial.wait_send()
    all_rows.wait_send()
    all_products.wait_send()
    stay.wait()
    gone = moved_out.at[pl.ds(0, WIDE - 1)]
    remote(gone, gone, s_mig, r_mig, (w, n)).wait()


def on_device(hidden, w_query, w_keyval, w_out, pool, page_req, page_idx, lengths, moves, accepted):
    dma = pltpu.SemaphoreType.DMA
    shape = jax.ShapeDtypeStruct
    page_shape = pool.shape[1:]
    leaving, pages, meta = pl.pallas_call(
        sort_kernel,
        out_shape=(
            shape((2, WIDE) + page_shape, BF16),
            shape(pool.shape, BF16),
            shape((8, 128), I32),
        ),
        in_specs=[SMEM_SPEC] * 4 + [ANY_SPEC],
        out_specs=(ANY_SPEC, ANY_SPEC, SMEM_SPEC),
        scratch_shapes=[pltpu.SMEM((WIDE,), I32), dma((2,))],
        name="sort_pages",
    )(moves.reshape(POOL), page_req, page_idx, lengths, pool)

    depth = hidden.shape[1]
    query, kvrow, kv, moved_a, meta_wide, meta_narrow = pl.pallas_call(
        gather_kernel,
        out_shape=(
            shape((4, WIDE * 8, HD), BF16),
            shape((8, 1024), BF16),
            shape((NARROW, 2, POOL, PAGE, HD), BF16),
            shape((WIDE,) + page_shape, BF16),
            shape((WIDE, 128), I32),
            shape((NARROW, 8, 128), I32),
        ),
        in_specs=[VMEM_SPEC] * 4 + [ANY_SPEC] * 2,
        out_specs=(VMEM_SPEC, VMEM_SPEC, ANY_SPEC, ANY_SPEC, VMEM_SPEC, VMEM_SPEC),
        scratch_shapes=[
            pltpu.VMEM((8, depth), BF16),
            pltpu.VMEM((WIDE, 8, depth), BF16),
            pltpu.VMEM((NARROW, 40, HD), F32),
            pltpu.VMEM((NARROW, 40, HD), F32),
            pltpu.VMEM((32, HD), BF16),
            pltpu.VMEM((4, 8, HD), BF16),
            pltpu.VMEM((WIDE, 8, HD), BF16),
            pltpu.VMEM((WIDE, 8, 128), I32),
            pltpu.VMEM((NARROW, 8, 128), I32),
            dma, dma, dma, dma, dma, dma, dma, dma,
            dma((3,)), dma, dma((3,)), dma, dma((4,)),
            dma, dma, dma, dma, dma, dma, dma, dma, dma, dma, dma, dma,
        ],
        compiler_params=pltpu.CompilerParams(collective_id=0, has_side_effects=True),
        name="spread_queries",
    )(hidden, w_query, w_keyval.T, meta, leaving, pages)

    rows = 4 * WIDE * STEPS
    width = CHUNK * PAGE
    chunks = NARROW * POOL // CHUNK
    partial, entries, moved_req, moved_idx = pl.pallas_call(
        attention_kernel,
        out_shape=(
            shape((WIDE + 1, 4, 8, HD), BF16),
            shape((1, STEPS, 1024), BF16),
            shape((POOL,), I32),
            shape((POOL,), I32),
        ),
        in_specs=[SMEM_SPEC] * 3 + [VMEM_SPEC] * 4,
        out_specs=(VMEM_SPEC, VMEM_SPEC, SMEM_SPEC, SMEM_SPEC),
        scratch_shapes=[
            pltpu.VMEM((rows, HD), BF16),
            pltpu.VMEM((chunks, 8, width), F32),
            pltpu.VMEM((chunks, rows, width), F32),
            pltpu.VMEM((rows, HD), F32),
            pltpu.VMEM((rows, 2 * HD), F32),
        ],
        compiler_params=pltpu.CompilerParams(vmem_limit_bytes=48 << 20),
        name="attend",
    )(meta_narrow[:, 2, 0:1], meta_wide, accepted, meta_narrow, query, kvrow, kv)

    attended, moved_b = pl.pallas_call(
        combine_kernel,
        out_shape=(
            shape((4 * STEPS, HD), BF16),
            shape((WIDE,) + page_shape, BF16),
        ),
        in_specs=[VMEM_SPEC] * 2 + [ANY_SPEC],
        out_specs=(VMEM_SPEC, ANY_SPEC),
        scratch_shapes=[
            pltpu.VMEM((WIDE + 1, 4, 8, HD), BF16),
            pltpu.VMEM((8, 4 * HD), BF16),
            pltpu.VMEM((WIDE, 8, 4 * HD), BF16),
            pltpu.VMEM((NARROW, 32, HD), BF16),
            pltpu.VMEM((NARROW, 32, HD), BF16),
            dma, dma, dma, dma, dma, dma, dma, dma, dma,
        ],
        compiler_params=pltpu.CompilerParams(collective_id=1, has_side_effects=True),
        name="combine",
    )(partial, w_out, leaving)
    moved = jnp.stack([moved_a, moved_b], axis=1).reshape(pool.shape)
    return attended, entries, moved, moved_req, moved_idx


def solution(mesh):
    in_specs = (
        P("wide", "narrow"),
        P("narrow", "wide"),
        P("narrow", "wide"),
        P("narrow", "wide"),
        P(("wide", "narrow"), None, None),
        P(("wide", "narrow")),
        P(("wide", "narrow")),
        P(),
        P(("wide", "narrow"), None),
        P(),
    )
    out_specs = (
        P("narrow", "wide"),
        P("wide", None, None),
        P(("wide", "narrow"), None, None),
        P(("wide", "narrow")),
        P(("wide", "narrow")),
    )
    return jax.shard_map(
        on_device, mesh=mesh, in_specs=in_specs, out_specs=out_specs, check_vma=False
    )
```

time: 758 us -> 258 us (0.34)
  blocking collectives: 374 us -> 0 us
  Pallas kernels: 0 us -> 246 us
  waiting for transfers between devices: 221 us -> 0 us
  local copies, waits for them, and re-layouts: 74.7 us -> 8.9 us
  matrix products: 24.9 us -> 0 us
  starting transfers between devices: 21.2 us -> 0 us
  other arithmetic: 20.5 us -> 1.42 us
  between operations: 15.9 us -> 0.71 us
    pallas_call x0 -> x4, Pallas kernels: none -> 246 us  [the longest x1 130 us: on_device(): pl.pallas_call(sort_kernel, out_shape=(shape((2, WIDE) + page_shape, BF16...]
    psum x1 -> x0, waiting for transfers between devices: 147 us -> none  [on_device(): lax.psum(part_sums.astype(jnp.bfloat16), 'wide').astype(jnp.float32)]
    all_gather x4 -> x0, blocking collectives: 144 us -> none  [the longest x1 77.1 us: on_device(): rows_all = lax.all_gather(hidden, 'wide', axis=0, tiled=True)]
    unnamed x3 -> x0, blocking collectives: 92.4 us -> none
    pmax x1 -> x0, blocking collectives: 79 us -> none  [on_device(): peak_all = lax.pmax(state[0], ('wide', 'narrow'))]
    all_gather x1 -> x0, waiting for transfers between devices: 62.4 us -> none  [on_device(): lax.all_gather(query_rows, 'wide', axis=1, tiled=True)]
    psum x1 -> x0, blocking collectives: 58.2 us -> none  [on_device(): lax.psum(part_totals.astype(jnp.bfloat16), 'wide').astype(jnp.float32)]
    dot_general x8 -> x0, matrix products: 24.9 us -> none  [the longest x1 8.17 us: on_device(): jnp.dot(selector, (sums * factor[..., None]).reshape(count, -1), precisio...]
  transfers between devices with their start and end apart: 6 -> 0, of which waited for: 4 -> 0; matrix products, arithmetic and copies ran while one was open for 4% -> 0% of each run, Pallas kernels for 0% -> 0%
where the time goes in v1:
time: 258 us; the launch traced here: 257 us
  Pallas kernels  246 us (95%)
  local copies, waits for them, and re-layouts  8.9 us (3%)
    pallas_call x1, Pallas kernels, on_device(): pl.pallas_call(sort_kernel, out_shape=(shape((2, WIDE) + page_shape, BF16...  130 us
    pallas_call x1, Pallas kernels, on_device(): pl.pallas_call(combine_kernel, out_shape=(shape((4 * STEPS, HD), BF16), s...  52.3 us
    pallas_call x1, Pallas kernels, on_device(): pl.pallas_call(gather_kernel, out_shape=(shape((4, WIDE * 8, HD), BF16),...  52.3 us
    pallas_call x1, Pallas kernels, on_device(): pl.pallas_call(attention_kernel, out_shape=(shape((WIDE + 1, 4, 8, HD), B...  11.9 us
    unnamed x19, local copies, waits for them, and re-layouts  6.64 us

profile of v1, /device:TPU:1, one launch (start us, length us, event | category | flops | bytes accessed | tf_op | source)
XLA Modules:
  0.0 257.1 jit_solution(12758690874968337545)
XLA Ops:
  0.6 129.7 %sort_pages.1 = (bf16[2,32,16,1024]{3,2,1,0:T(8,128)(2,1)}, bf16[64,16,1024]{2,1,0:T(8,128)(2,1)}, s32[8,128]{1,0:T(8,128)}) custom-call(s32[64]{0:T(128)} %bitcast.11, s32[64]{0:T(128)} %req.1, s32[64]{0:T(128)} %idx.1, s32[32]{0:T(128)} %lens.1, bf16[64,16,1024]{2,1,0:T(8,128)(2,1)} %pool.1), custom_call_target="tpu_custom_call" | custom-call | tf_op jit(solution)/shard_map/sort_pages/pallas_call | solution.py:551
  130.3 0.0 copy-start.6
  130.3 52.3 %spread_queries.1 = (bf16[4,256,128]{2,1,0:T(8,128)(2,1)}, bf16[8,1024]{1,0:T(8,128)(2,1)}, bf16[8,2,64,16,128]{4,3,2,1,0:T(8,128)(2,1)}, bf16[32,16,1024]{2,1,0...) custom-call(bf16[5,512]{1,0:T(8,128)(2,1)} %hidden.1, bf16[512,128]{1,0:T(8,128)(2,1)} %w_query.1, ...), custom_call_target="tpu_custom_call" | custom-call | tf_op jit(solution)/shard_map/spread_queries/pallas_call | solution.py:565
  182.6 0.8 slice.3
  183.3 0.0 copy-done.6
  183.3 0.0 copy-start
  183.4 2.2 copy-done
  185.5 0.0 copy-start.2
  185.5 0.9 copy-done.2
  186.5 0.0 copy-start.3
  186.5 0.8 copy-done.3
  187.2 0.0 copy-start.4
  187.2 0.7 copy-done.4
  188.0 0.0 copy-start.5
  188.0 0.7 copy-done.5
  188.7 11.9 %attend.1 = (bf16[33,4,8,128]{3,2,1,0:T(8,128)(2,1)S(1)}, bf16[1,5,1024]{2,1,0:T(8,128)(2,1)}, s32[64]{0:T(128)}, s32[64]{0:T(128)}) custom-call(s32[8,1]{1,0:T(8,128)S(1)} %bitcast.6, s32[32,128]{1,0:T(8,128)S(1)} %copy-done.5, s32[32]{0:T(128)S(1)} %copy-done.6, s32[8,8,128]{2,1,0:T(8,128)S(1)} %copy-done.3, bf16[4,256,128]{2,1,0:T(8,128)(2,1)S(1)} %copy-done.2, ...), custom_call_target="tpu_custom_call" | custom-call | tf_op jit(solution)/shard_map/attend/pallas_call | solution.py:598
  200.6 0.0 copy-start.1
  200.6 0.7 copy-done.1
  201.3 0.0 copy-start.7
  201.3 52.3 %combine.1 = (bf16[20,128]{1,0:T(8,128)(2,1)}, bf16[32,16,1024]{2,1,0:T(8,128)(2,1)}) custom-call(bf16[33,4,8,128]{3,2,1,0:T(8,128)(2,1)} %copy-done.1, bf16[512,128]{1,0:T(8,128)(2,1)} %w_out.1, bf16[2,32,16,1024]{3,2,1,0:T(8,128)(2,1)} %get-tuple-element.21.leaving), custom_call_target="tpu_custom_call" | custom-call | tf_op jit(solution)/shard_map/combine/pallas_call | solution.py:619
  253.6 0.0 copy-done.7
  253.6 1.4 pad_maximum_fusion
  255.0 0.0 copy-start.8
  255.1 1.5 copy.17
  256.5 0.0 copy-done.8
  256.6 0.6 copy.19
Async XLA Ops:
  130.3 53.0 %copy-start.6 = (s32[32]{0:T(128)S(1)}, s32[32]{0:T(128)}, u32[]{:S(2)}) copy-start(s32[32]{0:T(128)} %accepted.1) | copy-start | bytes 388
  183.3 2.2 copy-start
  185.5 0.9 copy-start.2
  186.5 0.8 copy-start.3
  187.2 0.7 copy-start.4
  188.0 0.7 copy-start.5
  200.6 0.7 copy-start.1
  201.3 52.3 %copy-start.7 = (bf16[32,16,1024]{2,1,0:T(8,128)(2,1)S(1)}, bf16[32,16,1024]{2,1,0:T(8,128)(2,1)}, u32[]{:S(2)}) copy-start(bf16[32,16,1024]{2,1,0:T(8,128)(2,1)} %get-tuple-element.31) | copy-start | bytes 3145732
  255.0 1.5 copy-start.8

commit v2 on v1

--- a/solution.py
+++ b/solution.py
@@ -31,7 +31,7 @@
 ANY_SPEC = pl.BlockSpec(memory_space=pl.ANY)
 
 
-def sort_kernel(moves, req, idx, lens, pool, sorted_out, live_out, meta, count, sem):
+def sort_kernel(moves, req, idx, lens, pool, first_out, second_out, live_out, meta, count):
     def clear(d, _):
         count[d] = 0
         return 0
@@ -45,12 +45,21 @@
         count[d] = k + 1
         r = req[p]
         i = idx[p]
-        pltpu.make_async_copy(pool.at[p], sorted_out.at[k, d], sem.at[0]).start()
+        page = pool[p]
+
+        @pl.when(k == 0)
+        def _():
+            first_out[d] = page
+
+        @pl.when(k != 0)
+        def _():
+            second_out[d] = page
+
         meta[0, 2 * d + k] = r
         meta[0, POOL + 2 * d + k] = i
         alive = r >= 0
         pos = jnp.where(alive, live, POOL - 1 - free)
-        pltpu.make_async_copy(pool.at[p], live_out.at[pos], sem.at[1]).start()
+        live_out[pos] = page
         seen = jnp.clip(lens[jnp.maximum(r, 0)] - i * PAGE, 0, PAGE)
         meta[1, pos] = r
         meta[1, POOL + pos] = jnp.where(alive, seen, 0)
@@ -59,8 +68,6 @@
 
     live, _ = lax.fori_loop(0, POOL, place, (jnp.int32(0), jnp.int32(0)))
     meta[2, 0] = live
-    pltpu.make_async_copy(live_out, live_out, sem.at[0]).wait()
-    pltpu.make_async_copy(live_out, live_out, sem.at[1]).wait()
 
 
 def enter(w, n):
@@ -143,11 +150,11 @@
 
     def send_page(k, _):
         peer = (w + k) % WIDE
-        remote(leaving.at[0, peer], moved_out.at[w], s_mig, r_mig, (peer, n)).start()
+        remote(leaving.at[peer], moved_out.at[w], s_mig, r_mig, (peer, n)).start()
         return 0
 
     lax.fori_loop(1, WIDE, send_page, 0)
-    stay = pltpu.make_async_copy(leaving.at[0, w], moved_out.at[w], l_sem.at[2])
+    stay = pltpu.make_async_copy(leaving.at[w], moved_out.at[w], l_sem.at[2])
     stay.start()
 
     def send_meta(k, _):
@@ -486,11 +493,11 @@
 
     def send_page(k, _):
         peer = (w + k) % WIDE
-        remote(leaving.at[1, peer], moved_out.at[w], s_mig, r_mig, (peer, n)).start()
+        remote(leaving.at[peer], moved_out.at[w], s_mig, r_mig, (peer, n)).start()
         return 0
 
     lax.fori_loop(1, WIDE, send_page, 0)
-    stay = pltpu.make_async_copy(leaving.at[1, w], moved_out.at[w], l_sem)
+    stay = pltpu.make_async_copy(leaving.at[w], moved_out.at[w], l_sem)
     stay.start()
     others = received.at[pl.ds(0, WIDE - 1)]
     all_partial = remote(others, others, s_d, r_d, (w, n))
@@ -548,16 +555,17 @@
     dma = pltpu.SemaphoreType.DMA
     shape = jax.ShapeDtypeStruct
     page_shape = pool.shape[1:]
-    leaving, pages, meta = pl.pallas_call(
+    first, second, pages, meta = pl.pallas_call(
         sort_kernel,
         out_shape=(
-            shape((2, WIDE) + page_shape, BF16),
+            shape((WIDE,) + page_shape, BF16),
+            shape((WIDE,) + page_shape, BF16),
             shape(pool.shape, BF16),
             shape((8, 128), I32),
         ),
-        in_specs=[SMEM_SPEC] * 4 + [ANY_SPEC],
-        out_specs=(ANY_SPEC, ANY_SPEC, SMEM_SPEC),
-        scratch_shapes=[pltpu.SMEM((WIDE,), I32), dma((2,))],
+        in_specs=[SMEM_SPEC] * 4 + [VMEM_SPEC],
+        out_specs=(VMEM_SPEC, VMEM_SPEC, VMEM_SPEC, SMEM_SPEC),
+        scratch_shapes=[pltpu.SMEM((WIDE,), I32)],
         name="sort_pages",
     )(moves.reshape(POOL), page_req, page_idx, lengths, pool)
 
@@ -590,7 +598,7 @@
         ],
         compiler_params=pltpu.CompilerParams(collective_id=0, has_side_effects=True),
         name="spread_queries",
-    )(hidden, w_query, w_keyval.T, meta, leaving, pages)
+    )(hidden, w_query, w_keyval.T, meta, first, pages)
 
     rows = 4 * WIDE * STEPS
     width = CHUNK * PAGE
@@ -634,7 +642,7 @@
         ],
         compiler_params=pltpu.CompilerParams(collective_id=1, has_side_effects=True),
         name="combine",
-    )(partial, w_out, leaving)
+    )(partial, w_out, second)
     moved = jnp.stack([moved_a, moved_b], axis=1).reshape(pool.shape)
     return attended, entries, moved, moved_req, moved_idx
 

time: 258 us -> 133 us (0.52)
  Pallas kernels: 246 us -> 121 us
    pallas_call x1, Pallas kernels: 130 us -> 5.88 us  [on_device(): pl.pallas_call(sort_kernel, out_shape=(shape((WIDE,) + page_shape, BF16),...]
where the time goes in v2:
time: 133 us; the launch traced here: 132 us
  Pallas kernels  121 us (91%)
  local copies, waits for them, and re-layouts  8.89 us (7%)
  other arithmetic  1.42 us (1%)
    pallas_call x1, Pallas kernels, on_device(): pl.pallas_call(gather_kernel, out_shape=(shape((4, WIDE * 8, HD), BF16),...  52.3 us
    pallas_call x1, Pallas kernels, on_device(): pl.pallas_call(combine_kernel, out_shape=(shape((4 * STEPS, HD), BF16), s...  51.3 us
    pallas_call x1, Pallas kernels, on_device(): pl.pallas_call(attention_kernel, out_shape=(shape((WIDE + 1, 4, 8, HD), B...  11.9 us
    unnamed x19, local copies, waits for them, and re-layouts  6.63 us
    pallas_call x1, Pallas kernels, on_device(): pl.pallas_call(sort_kernel, out_shape=(shape((WIDE,) + page_shape, BF16),...  5.88 us

profile of v2, /device:TPU:1, one launch (start us, length us, event | category | flops | bytes accessed | tf_op | source)
XLA Modules:
  0.0 132.4 jit_solution(12412652036112788265)
XLA Ops:
  0.6 5.9 %sort_pages.1 = (bf16[32,16,1024]{2,1,0:T(8,128)(2,1)}, bf16[32,16,1024]{2,1,0:T(8,128)(2,1)}, bf16[64,16,1024]{2,1,0:T(8,128)(2,1)}, s32[8,128]{1,0:T(8,128)}) custom-call(s32[64]{0:T(128)} %bitcast.11, s32[64]{0:T(128)} %req.1, s32[64]{0:T(128)} %idx.1, s32[32]{0:T(128)} %lens.1, bf16[64,16,1024]{2,1,0:T(8,128)(2,1)} %pool.1), custom_call_target="tpu_custom_call" | custom-call | tf_op jit(solution)/shard_map/sort_pages/pallas_call | solution.py:558
  6.5 0.0 copy-start.6
  6.5 52.3 %spread_queries.1 = (bf16[4,256,128]{2,1,0:T(8,128)(2,1)}, bf16[8,1024]{1,0:T(8,128)(2,1)}, bf16[8,2,64,16,128]{4,3,2,1,0:T(8,128)(2,1)}, bf16[32,16,1024]{2,1,0...) custom-call(bf16[5,512]{1,0:T(8,128)(2,1)} %hidden.1, bf16[512,128]{1,0:T(8,128)(2,1)} %w_query.1, ...), custom_call_target="tpu_custom_call" | custom-call | tf_op jit(solution)/shard_map/spread_queries/pallas_call | solution.py:573
  58.8 0.8 slice.3
  59.6 0.0 copy-done.6
  59.6 0.0 copy-start
  59.6 2.2 %copy-done = bf16[8,2,64,16,128]{4,3,2,1,0:T(8,128)(2,1)S(1)} copy-done((bf16[8,2,64,16,128]{4,3,2,1,0:T(8,128)(2,1)S(1)}, bf16[8,2,64,16,128]{4,3,2,1,0:T(8,128)(2,1)}, u32[]{:S(2)}) %copy-start) | copy-done | bytes 4194328
  61.7 0.0 copy-start.2
  61.7 0.9 copy-done.2
  62.7 0.0 copy-start.3
  62.7 0.8 copy-done.3
  63.5 0.0 copy-start.4
  63.5 0.7 copy-done.4
  64.2 0.0 copy-start.5
  64.2 0.7 copy-done.5
  64.9 0.0 copy-start.7
  64.9 11.9 %attend.1 = (bf16[33,4,8,128]{3,2,1,0:T(8,128)(2,1)S(1)}, bf16[1,5,1024]{2,1,0:T(8,128)(2,1)}, s32[64]{0:T(128)}, s32[64]{0:T(128)}) custom-call(s32[8,1]{1,0:T(8,128)S(1)} %bitcast.6, s32[32,128]{1,0:T(8,128)S(1)} %copy-done.5, s32[32]{0:T(128)S(1)} %copy-done.6, s32[8,8,128]{2,1,0:T(8,128)S(1)} %copy-done.3, bf16[4,256,128]{2,1,0:T(8,128)(2,1)S(1)} %copy-done.2, ...), custom_call_target="tpu_custom_call" | custom-call | tf_op jit(solution)/shard_map/attend/pallas_call | solution.py:606
  76.8 0.0 copy-start.1
  76.8 0.7 copy-done.1
  77.5 51.3 %combine.1 = (bf16[20,128]{1,0:T(8,128)(2,1)}, bf16[32,16,1024]{2,1,0:T(8,128)(2,1)}) custom-call(bf16[33,4,8,128]{3,2,1,0:T(8,128)(2,1)} %copy-done.1, bf16[512,128]{1,0:T(8,128)(2,1)} %w_out.1, bf16[32,16,1024]{2,1,0:T(8,128)(2,1)} %get-tuple-element.30.leaving), custom_call_target="tpu_custom_call" | custom-call | tf_op jit(solution)/shard_map/combine/pallas_call | solution.py:627
  128.9 0.0 copy-done.7
  128.9 1.4 %pad_maximum_fusion = bf16[32,2,16,1024]{3,2,0,1:T(8,128)(2,1)S(1)} fusion(bf16[32,1,16,1024]{3,2,0,1:T(8,128)(2,1)} %bitcast.9, bf16[32,1,16,1024]{3,2,0,1:T(8,128)(2,1)S(1)} %bitcast.8), kind=kLoop, calls=%fused_computation | loop fusion | flops 1048576 | bytes 4194304 | tf_op jit(solution)/shard_map/stack | solution.py:646
  130.3 0.0 copy-start.8
  130.3 1.5 %copy.17 = bf16[32,2,16,1024]{3,2,1,0:T(8,128)(2,1)} copy(bf16[32,2,16,1024]{3,2,0,1:T(8,128)(2,1)S(1)} %pad_maximum_fusion) | data formatting | bytes 4194304 | tf_op jit(solution)/shard_map/stack | solution.py:646
  131.8 0.0 copy-done.8
  131.8 0.6 copy.19
Async XLA Ops:
  6.5 53.0 %copy-start.6 = (s32[32]{0:T(128)S(1)}, s32[32]{0:T(128)}, u32[]{:S(2)}) copy-start(s32[32]{0:T(128)} %accepted.1) | copy-start | bytes 388
  59.6 2.2 %copy-start = (bf16[8,2,64,16,128]{4,3,2,1,0:T(8,128)(2,1)S(1)}, bf16[8,2,64,16,128]{4,3,2,1,0:T(8,128)(2,1)}, u32[]{:S(2)}) copy-start(bf16[8,2,64,16,128]{4,3,2,1,0:T(8,128)(2,1)} %get-tuple-element.28.kv) | copy-start | bytes 12582916
  61.7 0.9 copy-start.2
  62.7 0.8 copy-start.3
  63.5 0.7 copy-start.4
  64.2 0.7 copy-start.5
  64.9 64.0 %copy-start.7 = (bf16[32,16,1024]{2,1,0:T(8,128)(2,1)S(1)}, bf16[32,16,1024]{2,1,0:T(8,128)(2,1)}, u32[]{:S(2)}) copy-start(bf16[32,16,1024]{2,1,0:T(8,128)(2,1)} %get-tuple-element.33) | copy-start | bytes 3145732
  76.8 0.7 copy-start.1
  130.3 1.5 %copy-start.8 = (bf16[20,128]{1,0:T(8,128)(2,1)S(1)}, bf16[20,128]{1,0:T(8,128)(2,1)}, u32[]{:S(2)}) copy-start(bf16[20,128]{1,0:T(8,128)(2,1)} %get-tuple-element.42) | copy-start | bytes 15364

commit v3 on v1

v3 whole, which is shorter than its diff:
```python
import functools
import math

import jax
import jax.numpy as jnp
from jax import lax
from jax.experimental import pallas as pl
from jax.experimental.pallas import tpu as pltpu
from jax.sharding import PartitionSpec as P

HEADS = 32
KVH = 4
HD = 128
STEPS = 5
PAGE = 16
WIDE = 32
NARROW = 8
NY = 4
NZ = 8
POOL = 64
CHUNK = 32
EARLY = ((1, 0), (3, 0))
LATE = ((1, 1), (3, 1), (2, 0), (2, 1))
ORDER = (0, 1, 3, 2)
CUT1 = 5
CUT2 = 12
CUT3 = 12
SCALE = 1.0 / math.sqrt(HD)
LOG2E = 1.4426950408889634
NEG = -1e30
F32 = jnp.float32
BF16 = jnp.bfloat16
I32 = jnp.int32
MESH = pl.DeviceIdType.MESH
VMEM_SPEC = pl.BlockSpec(memory_space=pltpu.VMEM)
SMEM_SPEC = pl.BlockSpec(memory_space=pltpu.SMEM)
ANY_SPEC = pl.BlockSpec(memory_space=pl.ANY)


def order_kernel(moves, req, idx, lens, source, meta, count):
    def clear(d, _):
        count[d] = 0
        return 0

    lax.fori_loop(0, WIDE, clear, 0)

    def place(p, _):
        d = moves[p]
        k = count[d]
        count[d] = k + 1
        r = req[p]
        i = idx[p]
        source[2 * d + k] = p
        meta[0, 2 * d + k] = r
        meta[0, POOL + 2 * d + k] = i
        seen = jnp.clip(lens[jnp.maximum(r, 0)] - i * PAGE, 0, PAGE)
        meta[1, p] = r
        meta[1, POOL + p] = jnp.where(r >= 0, seen, 0)
        return 0

    lax.fori_loop(0, POOL, place, 0)


def enter(w, n):
    barrier = pltpu.get_barrier_semaphore()

    def wide_signal(k, _):
        pl.semaphore_signal(
            barrier, inc=1, device_id=((w + k) % WIDE, n), device_id_type=MESH
        )
        return 0

    def narrow_signal(k, _):
        pl.semaphore_signal(
            barrier, inc=1, device_id=(w, (n + k) % NARROW), device_id_type=MESH
        )
        return 0

    lax.fori_loop(1, WIDE, wide_signal, 0)
    lax.fori_loop(1, NARROW, narrow_signal, 0)
    pl.semaphore_wait(barrier, WIDE + NARROW - 2)


def remote(src, dst, send, recv, device):
    return pltpu.make_async_remote_copy(
        src_ref=src,
        dst_ref=dst,
        send_sem=send,
        recv_sem=recv,
        device_id=device,
        device_id_type=MESH,
    )


def payload_stats(peak, total, group, step):
    stat = jnp.where(group == step, peak, jnp.where(group - 8 == step, total, 0.0))
    first = stat.astype(BF16)
    rest = stat - first.astype(F32)
    second = rest.astype(BF16)
    third = (rest - second.astype(F32)).astype(BF16)
    return first, second, third


def whole_kernel(
    source, accepted, hidden, w_query, w_kv_t, w_out, meta, pool,
    attended, entries, moved_out, moved_req, moved_idx,
    hid_own, hid_all, part_q, part_kv, sum_q, sum_kv, query, kv_tiles, kv_four, kv_new,
    meta_w, meta_n, meta_s, pool_v, leaving, kv, pick, spread,
    token_req, scores, peaks, acc, partial, received, own, gathered, send_e, recv_e,
    s_a, r_a, s_m, r_m, s_mn, r_mn, s_mig, r_mig, l_sem, s_x, r_x, s_p, r_p,
    s_b, r_b, s_bk, r_bk, s_k1, r_k1, s_c2, r_c2, s_k2, r_k2, s_c3, r_c3,
    s_d, r_d, s_g, r_g, s_e, r_e,
):
    w = lax.axis_index("wide")
    n = lax.axis_index("narrow")
    z = w // NY
    y = w % NY
    x = n // 2
    c = n % 2
    other = 2 * x + (1 - c)
    rows = WIDE * STEPS
    load_pool = pltpu.make_async_copy(pool, pool_v, l_sem.at[0])
    load_pool.start()
    hid_own[...] = jnp.zeros_like(hid_own)
    hid_own[0:STEPS, :] = hidden[...]
    hid_all[pl.ds(w, 1)] = hid_own[...][None]
    meta_w[pl.ds(w, 1)] = meta[...][None]
    meta_n[pl.ds(n, 1)] = meta[...][None]
    enter(w, n)

    def send_hidden(k, _):
        remote(hid_own, hid_all.at[w], s_a, r_a, ((w + k) % WIDE, n)).start()
        return 0

    lax.fori_loop(1, WIDE, send_hidden, 0)

    def send_meta(k, _):
        remote(meta, meta_w.at[w], s_m, r_m, ((w + k) % WIDE, n)).start()
        return 0

    def send_meta_narrow(k, _):
        remote(meta, meta_n.at[n], s_mn, r_mn, (w, (n + k) % NARROW)).start()
        return 0

    lax.fori_loop(1, NARROW, send_meta_narrow, 0)

    def block_of(part, head):
        return pl.ds(pl.multiple_of(KVH * HD * part + HD * head, HD), HD)

    def exchange(dx, part):
        tx = (x + dx) % 4
        remote(
            pool.at[:, :, block_of(part, tx)],
            kv.at[n, part],
            s_x,
            r_x.at[dx - 1, part],
            (w, 2 * tx + c),
        ).start()

    own_copies = []
    for part in range(2):
        mine_here = pool.at[:, :, block_of(part, x)]
        remote(mine_here, kv.at[n, part], s_p, r_p.at[0], (w, other)).start()
        copy = pltpu.make_async_copy(mine_here, kv.at[n, part], l_sem.at[1 + part])
        copy.start()
        own_copies.append(copy)
    for dx, part in EARLY:
        exchange(dx, part)

    row = lax.broadcasted_iota(I32, (rows, WIDE * 8), 0).astype(F32)
    col = lax.broadcasted_iota(I32, (rows, WIDE * 8), 1).astype(F32)
    req_of_row = jnp.floor((row + 0.5) * 0.2)
    pick[...] = (col == req_of_row * 3.0 + row).astype(F32).astype(BF16)
    slot = lax.broadcasted_iota(I32, (WIDE * 8, rows), 0)
    req_of_slot = (slot >> 3).astype(F32)
    place = (slot & 7).astype(F32)
    origin = lax.broadcasted_iota(I32, (WIDE * 8, rows), 1).astype(F32)
    req_of_origin = jnp.floor((origin + 0.5) * 0.2)
    step_of_origin = origin - req_of_origin * 5.0
    same = req_of_slot == req_of_origin
    spread[0] = (same & (place == step_of_origin)).astype(F32).astype(BF16)
    for k in range(3):
        spread[1 + k] = (same & (place == 5.0 + k)).astype(F32).astype(BF16)
    peaks[...] = jnp.full(peaks.shape, NEG, F32)
    acc[...] = jnp.zeros_like(acc)

    load_pool.wait()

    def take_page(j, _):
        leaving[j] = pool_v[source[j]]
        return 0

    lax.fori_loop(0, POOL, take_page, 0)
    stay = pltpu.make_async_copy(
        leaving.at[pl.ds(2 * w, 2)], moved_out.at[pl.ds(2 * w, 2)], l_sem.at[3]
    )
    stay.start()

    def send_pages(first, last):
        def send_pair(i, _):
            for k in (i, WIDE - i):
                peer = (w + k) % WIDE
                remote(
                    leaving.at[pl.ds(2 * peer, 2)],
                    moved_out.at[pl.ds(2 * w, 2)],
                    s_mig,
                    r_mig,
                    (peer, n),
                ).start()
            return 0

        lax.fori_loop(first, min(last, 16), send_pair, 0)
        if first <= 16 < last:
            peer = (w + 16) % WIDE
            remote(
                leaving.at[pl.ds(2 * peer, 2)],
                moved_out.at[pl.ds(2 * w, 2)],
                s_mig,
                r_mig,
                (peer, n),
            ).start()

    others = hid_all.at[pl.ds(0, WIDE - 1)]
    all_hidden = remote(others, others, s_a, r_a, (w, n))
    all_hidden.wait_recv()
    padded = hid_all[...].reshape(WIDE * 8, hid_all.shape[2])
    packed = jnp.dot(pick[...], padded, preferred_element_type=F32).astype(BF16)
    part_q[...] = jnp.dot(packed, w_query[...], preferred_element_type=F32)
    to_hub_q = remote(part_q, sum_q.at[n], s_b, r_b, (w, z))
    to_hub_kv = remote(part_kv, sum_kv.at[n], s_bk, r_bk, (w, z))

    @pl.when(n != z)
    def _():
        to_hub_q.start()

    new_kv = lax.dot_general(
        padded, w_kv_t[...], (((1,), (1,)), ((), ())), preferred_element_type=F32
    )
    for j in range(4):
        part_kv[:, 32 * j : 32 * j + 32] = new_kv[64 * j : 64 * j + 64]

    @pl.when(n != z)
    def _():
        to_hub_kv.start()

    for dx, part in LATE:
        exchange(dx, part)
    lax.fori_loop(1, WIDE, send_meta, 0)
    send_pages(1, CUT1)
    mine = query.at[y]
    seven_q = sum_q.at[pl.ds(0, 7)]
    seven_kv = sum_kv.at[pl.ds(0, 7)]

    @pl.when(n == z)
    def _():
        sum_q[pl.ds(n, 1)] = part_q[...][None]
        remote(seven_q, seven_q, s_b, r_b, (w, n)).wait_recv()
        query[pl.ds(y, 1)] = jnp.sum(sum_q[...], axis=0).astype(BF16)[None]

        def send_query(k, _):
            peer = ((z + k) % NZ) * NY + y
            remote(mine, mine, s_c2, r_c2, (peer, n)).start()
            return 0

        lax.fori_loop(1, NZ, send_query, 0)

    @pl.when(n != z)
    def _():
        remote(mine, mine, s_c2, r_c2, (w, n)).wait_recv()

    for dy in (1, 3, 2):
        remote(mine, mine, s_c3, r_c3, (z * NY + (y + dy) % NY, n)).start()

    @pl.when(n == z)
    def _():
        sum_kv[pl.ds(n, 1)] = part_kv[...][None]
        remote(seven_kv, seven_kv, s_bk, r_bk, (w, n)).wait_recv()
        kv_tiles[...] = jnp.sum(sum_kv[...], axis=0).astype(BF16).reshape(8, 8, HD)
        kv_four[pl.ds(y, 1)] = kv_tiles[pl.ds(w % 8, 1)]

        def send_tile(k, _):
            peer = (w + k) % WIDE
            remote(kv_tiles.at[peer % 8], kv_four.at[y], s_k1, r_k1, (peer, n)).start()
            return 0

        lax.fori_loop(1, WIDE, send_tile, 0)

    send_pages(CUT1, CUT2)

    def relay(dx):
        arrived = 2 * ((x + 4 - dx) % 4) + c
        for part in range(2):
            here = kv.at[arrived, part]
            remote(here, here, s_x, r_x.at[dx - 1, part], (w, n)).wait_recv()
        here = kv.at[arrived]
        remote(here, here, s_p, r_p.at[dx], (w, other)).start()

    relay(1)
    relay(3)
    narrow_tiles = meta_n.at[pl.ds(0, NARROW - 1)]
    remote(narrow_tiles, narrow_tiles, s_mn, r_mn, (w, n)).wait()
    page_meta = meta_n[:, 1, :].astype(F32).astype(BF16)
    page = lax.broadcasted_iota(I32, (2 * POOL, POOL * PAGE), 0)
    page_of = lax.broadcasted_iota(I32, (2 * POOL, POOL * PAGE), 1) >> 4
    spread_req = (page == page_of).astype(F32).astype(BF16)
    spread_seen = (page - POOL == page_of).astype(F32).astype(BF16)
    owner = jnp.dot(page_meta, spread_req, preferred_element_type=F32)
    seen = jnp.dot(page_meta, spread_seen, preferred_element_type=F32)
    within = (lax.broadcasted_iota(I32, (NARROW, POOL * PAGE), 1) & 15).astype(F32)
    owner = jnp.where(within < seen, owner, -1.0)
    width = CHUNK * PAGE
    per = POOL // CHUNK
    for s in range(NARROW):
        for i in range(per):
            token_req[per * s + i] = jnp.broadcast_to(
                owner[s : s + 1, width * i : width * i + width], (8, width)
            )
    all_row = lax.broadcasted_iota(I32, (rows, 1), 0).astype(F32)
    row_req = jnp.floor((all_row + 0.5) * 0.2)
    row_req = jnp.concatenate([row_req] * 4, axis=0)
    three = query.at[pl.ds(0, 3)]
    spread_query = remote(three, three, s_c3, r_c3, (w, n))
    spread_query.wait_recv()

    for copy in own_copies:
        copy.wait()
    for g, dx in enumerate(ORDER):
        if dx == 2:
            relay(2)
        from_other = kv.at[2 * ((x + 4 - dx) % 4) + (1 - c)]
        remote(from_other, from_other, s_p, r_p.at[dx], (w, n)).wait_recv()

        def score(j, _, g=g, dx=dx):
            s = 2 * ((x + 4 - dx) % 4) + j // per
            i = j % per
            keys = kv[s, 0, pl.ds(i * CHUNK, CHUNK)].reshape(width, HD)
            raw = lax.dot_general(
                query[...].reshape(4 * rows, HD),
                keys,
                (((1,), (1,)), ((), ())),
                preferred_element_type=F32,
            )
            owners = token_req[per * s + i][0:1, :]
            raw = jnp.where(row_req == owners, raw, NEG)
            scores[2 * per * g + j] = raw
            top = raw[:, 0:HD]
            for t in range(1, width // HD):
                top = jnp.maximum(top, raw[:, HD * t : HD * t + HD])
            peaks[...] = jnp.maximum(peaks[...], top)
            return 0

        lax.fori_loop(0, 2 * per, score, 0)

    peak = jnp.max(peaks[...], axis=1, keepdims=True)
    ones = jnp.ones((width, HD), BF16)
    for g, dx in enumerate(ORDER):

        def weigh(j, _, g=g, dx=dx):
            s = 2 * ((x + 4 - dx) % 4) + j // per
            i = j % per
            values = kv[s, 1, pl.ds(i * CHUNK, CHUNK)].reshape(width, HD)
            weights = jnp.exp2(
                (scores[2 * per * g + j] - peak) * (SCALE * LOG2E)
            ).astype(BF16)
            acc[...] += jnp.dot(
                weights, jnp.concatenate([values, ones], axis=1), preferred_element_type=F32
            )
            return 0

        lax.fori_loop(0, 2 * per, weigh, 0)

    group = (lax.broadcasted_iota(I32, (rows, HD), 1) >> 3).astype(F32)
    srow = lax.broadcasted_iota(I32, (rows, HD), 0).astype(F32)
    step_of = srow - jnp.floor((srow + 0.5) * 0.2) * 5.0
    for h in range(4):
        here = slice(rows * h, rows * h + rows)
        terms = payload_stats(peak[here] * SCALE, acc[here, HD:], group, step_of)
        laid = jnp.dot(spread[0], acc[here, 0:HD].astype(BF16), preferred_element_type=F32)
        for k in range(3):
            laid += jnp.dot(spread[1 + k], terms[k], preferred_element_type=F32)
        partial[:, h] = laid.astype(BF16).reshape(WIDE, 8, HD)

    def send_partial(k, _):
        peer = (w + k) % WIDE
        remote(partial.at[peer], received.at[w], s_d, r_d, (peer, n)).start()
        return 0

    lax.fori_loop(1, WIDE, send_partial, 0)
    received[pl.ds(w, 1)] = partial[pl.ds(w, 1)]
    send_pages(CUT2, CUT3)

    four_tiles = kv_four
    three_tiles = kv_four.at[pl.ds(0, 3)]

    @pl.when(n != z)
    def _():
        remote(four_tiles, four_tiles, s_k1, r_k1, (w, n)).wait_recv()

    @pl.when(n == z)
    def _():
        remote(three_tiles, three_tiles, s_k1, r_k1, (w, n)).wait_recv()

    lane = lax.broadcasted_iota(I32, (8, HD), 1)
    merged = jnp.zeros((8, HD), F32)
    for t in range(4):
        turned = pltpu.roll(kv_four[t].astype(F32), (t + 4 - w // 8) % 4 * 32, 1)
        merged = merged + jnp.where((lane >= 32 * t) & (lane < 32 * t + 32), turned, 0.0)
    kv_new[pl.ds(n, 1)] = merged.astype(BF16)[None]

    def send_new(k, _):
        remote(kv_new.at[n], kv_new.at[n], s_k2, r_k2, (w, (n + k) % NARROW)).start()
        return 0

    lax.fori_loop(1, NARROW, send_new, 0)
    wide_tiles = meta_w.at[pl.ds(0, WIDE - 1)]
    remote(wide_tiles, wide_tiles, s_m, r_m, (w, n)).wait()
    to_scalar = pltpu.make_async_copy(meta_w.at[:, 0], meta_s, l_sem.at[4])
    to_scalar.start()
    to_scalar.wait()

    def moved_meta(i, _):
        for k in range(2):
            moved_req[2 * i + k] = meta_s[i, 2 * w + k]
            moved_idx[2 * i + k] = meta_s[i, POOL + 2 * w + k]
        return 0

    lax.fori_loop(0, WIDE, moved_meta, 0)
    seven_new = kv_new.at[pl.ds(0, 7)]
    remote(seven_new, seven_new, s_k2, r_k2, (w, n)).wait()
    step = lax.broadcasted_iota(I32, (STEPS, HD), 0)
    for b in range(8):
        entries[0, :, HD * b : HD * b + HD] = jnp.where(
            step < accepted[w], kv_new[b][0:STEPS, :].astype(F32), 0.0
        ).astype(BF16)

    first_row = lax.broadcasted_iota(I32, (32, rows), 0)
    from_row = lax.broadcasted_iota(I32, (32, rows), 1)
    ours = (from_row == 5 * w + (first_row & 7)) & ((first_row & 7) < STEPS)
    ours = ours.astype(F32).astype(BF16)
    k_new = kv_new[x]
    v_new = kv_new[KVH + x]
    sub = lax.broadcasted_iota(I32, (8, HD), 0)
    lane_group = lane >> 3
    fresh_row = lax.broadcasted_iota(I32, (8, 8), 0)
    fresh_key = lax.broadcasted_iota(I32, (8, 8), 1)
    known = fresh_key <= fresh_row
    for h in range(4):
        q_new = jnp.dot(ours[0:8], query[h], preferred_element_type=F32).astype(BF16)
        fresh = lax.dot_general(
            q_new, k_new, (((1,), (1,)), ((), ())), preferred_element_type=F32
        ) * SCALE
        fresh = jnp.where(known, fresh, NEG)
        fresh_peak = jnp.max(fresh, axis=1, keepdims=True)
        fresh_weight = jnp.where(known, jnp.exp(fresh - fresh_peak), 0.0)
        fresh_total = jnp.sum(fresh_weight, axis=1, keepdims=True)
        fresh_sum = jnp.dot(fresh_weight.astype(BF16), v_new, preferred_element_type=F32)
        stat = jnp.where(
            lane_group == sub,
            fresh_peak,
            jnp.where(lane_group - 8 == sub, fresh_total, 0.0),
        )
        line = jnp.sum(jnp.where(sub < STEPS, stat, 0.0), axis=0, keepdims=True)
        first = line.astype(BF16).astype(F32)
        second = (line - first).astype(BF16).astype(F32)
        third = line - first - second
        tile = jnp.where(
            sub < STEPS,
            fresh_sum,
            jnp.where(sub == 5, first, jnp.where(sub == 6, second, third)),
        )
        received[WIDE, h] = tile.astype(BF16)

    others = received.at[pl.ds(0, WIDE - 1)]
    all_partial = remote(others, others, s_d, r_d, (w, n))
    all_partial.wait_recv()
    sub3 = lax.broadcasted_iota(I32, (1, 8, HD), 1)
    group3 = lax.broadcasted_iota(I32, (1, 8, HD), 2) >> 3
    for h in range(4):
        tiles = received[:, h].astype(F32)
        line = (tiles[:, 7:8] + tiles[:, 6:7]) + tiles[:, 5:6]
        high = jnp.max(jnp.where(group3 == sub3, line, -3e38), axis=2, keepdims=True)
        total = jnp.max(jnp.where(group3 - 8 == sub3, line, 0.0), axis=2, keepdims=True)
        top = jnp.max(high, axis=0, keepdims=True)
        factor = jnp.exp(high - top)
        total = jnp.sum(factor * total, axis=0)
        sums = jnp.sum(factor * tiles, axis=0)
        own[:, HD * h : HD * h + HD] = jnp.where(
            sub < STEPS, sums / jnp.where(sub < STEPS, total, 1.0), 0.0
        ).astype(BF16)
    gathered[pl.ds(w, 1)] = own[...][None]

    def send_own(k, _):
        remote(own, gathered.at[w], s_g, r_g, ((w + k) % WIDE, n)).start()
        return 0

    lax.fori_loop(1, WIDE, send_own, 0)
    send_pages(CUT3, 17)
    others = gathered.at[pl.ds(0, WIDE - 1)]
    all_rows = remote(others, others, s_g, r_g, (w, n))
    all_rows.wait_recv()
    attn = gathered[...].reshape(WIDE * 8, gathered.shape[2])
    product = jnp.dot(attn, w_out[...], preferred_element_type=F32)
    send_e[...] = product.astype(BF16).reshape(NARROW, 32, HD)
    recv_e[pl.ds(n, 1)] = send_e[pl.ds(n, 1)]

    def send_product(k, _):
        peer = (n + k) % NARROW
        remote(send_e.at[peer], recv_e.at[n], s_e, r_e, (w, peer)).start()
        return 0

    lax.fori_loop(1, NARROW, send_product, 0)
    others = recv_e.at[pl.ds(0, NARROW - 1)]
    all_products = remote(others, others, s_e, r_e, (w, n))
    all_products.wait_recv()
    result = jnp.sum(recv_e[...].astype(F32), axis=0)
    for j in range(4):
        attended[STEPS * j : STEPS * j + STEPS, :] = result[8 * j : 8 * j + STEPS].astype(BF16)

    all_hidden.wait_send()
    spread_query.wait_send()
    three = kv.at[pl.ds(0, 3)]
    remote(three, three, s_x, r_x.at[0, 0], (w, n)).wait_send()
    four = kv.at[pl.ds(0, 4)]
    remote(four, four, s_p, r_p.at[0], (w, n)).wait_send()

    @pl.when(n != z)
    def _():
        to_hub_q.wait_send()
        to_hub_kv.wait_send()

    tiles31 = received.at[pl.ds(0, 31), 0]

    @pl.when(n == z)
    def _():
        remote(tiles31, tiles31, s_k1, r_k1, (w, n)).wait_send()
        four_q = query
        three_q = query.at[pl.ds(0, 3)]
        remote(four_q, four_q, s_c2, r_c2, (w, n)).wait_send()
        remote(three_q, three_q, s_c2, r_c2, (w, n)).wait_send()

    all_partial.wait_send()
    all_rows.wait_send()
    all_products.wait_send()
    stay.wait()
    gone = moved_out.at[pl.ds(0, POOL - 2)]
    remote(gone, gone, s_mig, r_mig, (w, n)).wait()


def on_device(hidden, w_query, w_keyval, w_out, pool, page_req, page_idx, lengths, moves, accepted):
    dma = pltpu.SemaphoreType.DMA
    shape = jax.ShapeDtypeStruct
    source, meta = pl.pallas_call(
        order_kernel,
        out_shape=(shape((POOL,), I32), shape((8, 128), I32)),
        in_specs=[SMEM_SPEC] * 4,
        out_specs=(SMEM_SPEC, SMEM_SPEC),
        scratch_shapes=[pltpu.SMEM((WIDE,), I32)],
        name="order_pages",
    )(moves.reshape(POOL), page_req, page_idx, lengths)

    depth = hidden.shape[1]
    rows = WIDE * STEPS
    width = CHUNK * PAGE
    chunks = NARROW * POOL // CHUNK
    attended, entries, moved, moved_req, moved_idx = pl.pallas_call(
        whole_kernel,
        out_shape=(
            shape((4 * STEPS, HD), BF16),
            shape((1, STEPS, 1024), BF16),
            shape(pool.shape, BF16),
            shape((POOL,), I32),
            shape((POOL,), I32),
        ),
        in_specs=[SMEM_SPEC] * 2 + [VMEM_SPEC] * 5 + [ANY_SPEC],
        out_specs=(VMEM_SPEC, VMEM_SPEC, ANY_SPEC, SMEM_SPEC, SMEM_SPEC),
        scratch_shapes=[
            pltpu.VMEM((8, depth), BF16),
            pltpu.VMEM((WIDE, 8, depth), BF16),
            pltpu.VMEM((rows, HD), F32),
            pltpu.VMEM((64, HD), F32),
            pltpu.VMEM((NARROW, rows, HD), F32),
            pltpu.VMEM((NARROW, 64, HD), F32),
            pltpu.VMEM((4, rows, HD), BF16),
            pltpu.VMEM((8, 8, HD), BF16),
            pltpu.VMEM((4, 8, HD), BF16),
            pltpu.VMEM((8, 8, HD), BF16),
            pltpu.VMEM((WIDE, 8, 128), I32),
            pltpu.VMEM((NARROW, 8, 128), I32),
            pltpu.SMEM((WIDE, 128), I32),
            pltpu.VMEM(pool.shape, BF16),
            pltpu.VMEM(pool.shape, BF16),
            pltpu.VMEM((NARROW, 2, POOL, PAGE, HD), BF16),
            pltpu.VMEM((rows, WIDE * 8), BF16),
            pltpu.VMEM((4, WIDE * 8, rows), BF16),
            pltpu.VMEM((chunks, 8, width), F32),
            pltpu.VMEM((chunks, 4 * rows, width), F32),
            pltpu.VMEM((4 * rows, HD), F32),
            pltpu.VMEM((4 * rows, 2 * HD), F32),
            pltpu.VMEM((WIDE, 4, 8, HD), BF16),
            pltpu.VMEM((WIDE + 1, 4, 8, HD), BF16),
            pltpu.VMEM((8, 4 * HD), BF16),
            pltpu.VMEM((WIDE, 8, 4 * HD), BF16),
            pltpu.VMEM((NARROW, 32, HD), BF16),
            pltpu.VMEM((NARROW, 32, HD), BF16),
            dma, dma, dma, dma, dma, dma, dma, dma,
            dma((5,)), dma, dma((3, 2)), dma, dma((4,)),
            dma, dma, dma, dma, dma, dma, dma, dma, dma, dma, dma, dma,
            dma, dma, dma, dma, dma, dma,
        ],
        compiler_params=pltpu.CompilerParams(
            collective_id=0, has_side_effects=True, vmem_limit_bytes=50 << 20
        ),
        name="verify_step",
    )(source, accepted, hidden, w_query, w_keyval.T, w_out, meta, pool)
    return attended, entries, moved, moved_req, moved_idx


def solution(mesh):
    in_specs = (
        P("wide", "narrow"),
        P("narrow", "wide"),
        P("narrow", "wide"),
        P("narrow", "wide"),
        P(("wide", "narrow"), None, None),
        P(("wide", "narrow")),
        P(("wide", "narrow")),
        P(),
        P(("wide", "narrow"), None),
        P(),
    )
    out_specs = (
        P("narrow", "wide"),
        P("wide", None, None),
        P(("wide", "narrow"), None, None),
        P(("wide", "narrow")),
        P(("wide", "narrow")),
    )
    return jax.shard_map(
        on_device, mesh=mesh, in_specs=in_specs, out_specs=out_specs, check_vma=False
    )
```

time: 258 us -> 119 us (0.46)
  Pallas kernels: 246 us -> 110 us
    pallas_call x4 -> x2, Pallas kernels: 246 us -> 110 us  [the longest x1 107 us: on_device(): pl.pallas_call(whole_kernel, out_shape=(shape((4 * STEPS, HD), BF16), sha...]
where the time goes in v3:
time: 119 us
  Pallas kernels  110 us (92%)
  local copies, waits for them, and re-layouts  8.79 us (7%)
    pallas_call x1, Pallas kernels, on_device(): pl.pallas_call(whole_kernel, out_shape=(shape((4 * STEPS, HD), BF16), sha...  107 us
    unnamed x19, local copies, waits for them, and re-layouts  8.79 us
    pallas_call x1, Pallas kernels, on_device(): pl.pallas_call(order_kernel, out_shape=(shape((POOL,), I32), shape((8, 12...  2.51 us

profile of v3, /device:TPU:1, one launch (start us, length us, event | category | flops | bytes accessed | tf_op | source)
XLA Modules:
  0.0 119.1 jit_solution(15810192223546807419)
XLA Ops:
  0.6 2.5 %order_pages.1 = (s32[64]{0:T(128)}, s32[8,128]{1,0:T(8,128)}) custom-call(s32[64]{0:T(128)} %bitcast.3, s32[64]{0:T(128)} %req.1, s32[64]{0:T(128)} %idx.1, s32[32]{0:T(128)} %lens.1), custom_call_target="tpu_custom_call" | custom-call | tf_op jit(solution)/shard_map/order_pages/pallas_call | solution.py:552
  3.1 0.0 copy-start
  3.2 0.9 copy-done
  4.1 0.0 copy-start.1
  4.1 0.9 copy-done.1
  5.0 0.0 copy-start.2
  5.0 0.8 copy-done.2
  5.7 0.0 copy-start.3
  5.7 0.7 copy-done.3
  6.4 0.0 copy-start.4
  6.4 0.7 copy-done.4
  7.1 0.0 copy-start.5
  7.1 0.7 copy-done.5
  7.8 0.0 copy-start.6
  7.8 0.7 copy-done.6
  8.4 107.1 %verify_step.1 = (bf16[20,128]{1,0:T(8,128)(2,1)S(1)}, bf16[1,5,1024]{2,1,0:T(8,128)(2,1)S(1)}, bf16[64,16,1024]{2,1,0:T(8,128)(2,1)S(1)}, s32[64]{0:T(128)S(1)}, s32[64]{0:T(128)S(1)}) custom-call(s32[64]{0:T(128)S(1)} %copy-done.6, s32[32]{0:T(128)S(1)} %copy-done.5, bf16[5,512]{1,0:T(8,128)(2,1)S(1)} %copy-done.3, bf16[512,128]{1,0:T(8,128)(2,1)S(1)} %copy-done, ...), custom_call_target="tpu_custom_call" | custom-call | tf_op jit(solution)/shard_map/verify_step/pallas_call | solution.py:565
  115.5 0.6 copy.20
  116.1 0.6 copy.21
  116.7 1.3 %copy.22 = bf16[64,16,1024]{2,1,0:T(8,128)(2,1)} copy(bf16[64,16,1024]{2,1,0:T(8,128)(2,1)S(1)} %get-tuple-element.16) | data formatting | bytes 4194304
  118.1 0.5 copy.23
  118.6 0.5 copy.24
Async XLA Ops:
  3.1 0.9 copy-start
  4.1 0.9 copy-start.1
  5.0 0.8 copy-start.2
  5.7 0.7 copy-start.3
  6.4 0.7 copy-start.4
  7.1 0.7 copy-start.5
  7.8 0.7 copy-start.6

commit v4 on v3

--- a/solution.py
+++ b/solution.py
@@ -19,12 +19,13 @@
 NZ = 8
 POOL = 64
 CHUNK = 32
-EARLY = ((1, 0), (3, 0))
-LATE = ((1, 1), (3, 1), (2, 0), (2, 1))
-ORDER = (0, 1, 3, 2)
-CUT1 = 5
-CUT2 = 12
-CUT3 = 12
+PIECES = 4
+EARLY = ((2, 0), (1, 0), (3, 0))
+LATE = ((2, 1), (1, 1), (3, 1))
+ORDER = (0, 2, 1, 3)
+CUT1 = 8
+CUT2 = 14
+CUT3 = 14
 SCALE = 1.0 / math.sqrt(HD)
 LOG2E = 1.4426950408889634
 NEG = -1e30
@@ -37,32 +38,7 @@
 ANY_SPEC = pl.BlockSpec(memory_space=pl.ANY)
 
 
-def order_kernel(moves, req, idx, lens, source, meta, count):
-    def clear(d, _):
-        count[d] = 0
-        return 0
-
-    lax.fori_loop(0, WIDE, clear, 0)
-
-    def place(p, _):
-        d = moves[p]
-        k = count[d]
-        count[d] = k + 1
-        r = req[p]
-        i = idx[p]
-        source[2 * d + k] = p
-        meta[0, 2 * d + k] = r
-        meta[0, POOL + 2 * d + k] = i
-        seen = jnp.clip(lens[jnp.maximum(r, 0)] - i * PAGE, 0, PAGE)
-        meta[1, p] = r
-        meta[1, POOL + p] = jnp.where(r >= 0, seen, 0)
-        return 0
-
-    lax.fori_loop(0, POOL, place, 0)
-
-
-def enter(w, n):
-    barrier = pltpu.get_barrier_semaphore()
+def greet(w, n, barrier):
 
     def wide_signal(k, _):
         pl.semaphore_signal(
@@ -78,7 +54,6 @@
 
     lax.fori_loop(1, WIDE, wide_signal, 0)
     lax.fori_loop(1, NARROW, narrow_signal, 0)
-    pl.semaphore_wait(barrier, WIDE + NARROW - 2)
 
 
 def remote(src, dst, send, recv, device):
@@ -102,13 +77,14 @@
 
 
 def whole_kernel(
-    source, accepted, hidden, w_query, w_kv_t, w_out, meta, pool,
+    moves, page_req, page_idx, lengths, accepted, hidden, w_query_in, w_kv_in, w_out_in, pool,
     attended, entries, moved_out, moved_req, moved_idx,
+    small, small_len, hid_in, w_query, w_kv_t, w_out, meta, source_v, source,
     hid_own, hid_all, part_q, part_kv, sum_q, sum_kv, query, kv_tiles, kv_four, kv_new,
-    meta_w, meta_n, meta_s, pool_v, leaving, kv, pick, spread,
+    meta_n, pool_v, leaving, kv, pick, spread,
     token_req, scores, peaks, acc, partial, received, own, gathered, send_e, recv_e,
-    s_a, r_a, s_m, r_m, s_mn, r_mn, s_mig, r_mig, l_sem, s_x, r_x, s_p, r_p,
-    s_b, r_b, s_bk, r_bk, s_k1, r_k1, s_c2, r_c2, s_k2, r_k2, s_c3, r_c3,
+    l_in, s_a, r_a, s_mn, r_mn, s_mig, r_mig, l_sem, s_x, r_x, s_p, r_p,
+    s_b, r_b, s_bk, r_bk, s_k1, r_k1, s_k3, r_k3, s_c2, r_c2, s_k2, r_k2, s_c3, r_c3,
     s_d, r_d, s_g, r_g, s_e, r_e,
 ):
     w = lax.axis_index("wide")
@@ -119,30 +95,75 @@
     c = n % 2
     other = 2 * x + (1 - c)
     rows = WIDE * STEPS
-    load_pool = pltpu.make_async_copy(pool, pool_v, l_sem.at[0])
-    load_pool.start()
+    loads = []
+    for i, (origin, target) in enumerate(
+        (
+            (moves, small.at[0]),
+            (page_req, small.at[1]),
+            (page_idx, small.at[2]),
+            (lengths, small_len.at[0]),
+            (accepted, small_len.at[1]),
+            (hidden, hid_in),
+            (pool, pool_v),
+            (w_query_in, w_query),
+            (w_kv_in, w_kv_t),
+            (w_out_in, w_out),
+        )
+    ):
+        loads.append(pltpu.make_async_copy(origin, target, l_in.at[i]))
+        loads[-1].start()
+    barrier = pltpu.get_barrier_semaphore()
+    greet(w, n, barrier)
+    for load in loads[0:6]:
+        load.wait()
     hid_own[...] = jnp.zeros_like(hid_own)
-    hid_own[0:STEPS, :] = hidden[...]
+    hid_own[0:STEPS, :] = hid_in[...]
+    sub64 = lax.broadcasted_iota(I32, (POOL, POOL), 0).astype(F32)
+    lane64 = lax.broadcasted_iota(I32, (POOL, POOL), 1).astype(F32)
+    diagonal = sub64 == lane64
+
+    def as_column(line):
+        return jnp.sum(jnp.where(diagonal, line, 0.0), axis=1, keepdims=True)
+
+    leave = small[0].astype(F32)
+    leave_column = as_column(leave)
+    earlier = (leave_column == leave) & (lane64 < sub64)
+    rank = jnp.sum(earlier.astype(F32), axis=1, keepdims=True)
+    taken = leave_column * 2.0 + rank == lane64
+    req_line = small[1].astype(F32)
+    idx_line = small[2].astype(F32)
+
+    def reorder(line):
+        return jnp.sum(jnp.where(taken, as_column(line), 0.0), axis=0, keepdims=True)
+
+    source_row = jnp.sum(jnp.where(taken, sub64, 0.0), axis=0, keepdims=True).astype(I32)
+    source_v[...] = jnp.zeros_like(source_v)
+    source_v[0:1, 0:POOL] = source_row
+    sub32 = lax.broadcasted_iota(I32, (WIDE, WIDE), 0)
+    lane32 = lax.broadcasted_iota(I32, (WIDE, WIDE), 1)
+    len_column = jnp.sum(
+        jnp.where(sub32 == lane32, small_len[0].astype(F32), 0.0), axis=1, keepdims=True
+    )
+    owner_is = lax.broadcasted_iota(I32, (WIDE, POOL), 0).astype(F32) == req_line
+    length_of = jnp.sum(jnp.where(owner_is, len_column, 0.0), axis=0, keepdims=True)
+    seen_line = jnp.clip(length_of - idx_line * PAGE, 0.0, float(PAGE))
+    seen_line = jnp.where(req_line >= 0.0, seen_line, 0.0)
+    meta[...] = jnp.zeros_like(meta)
+    idx_high = jnp.floor(idx_line * (1.0 / 16.0))
+    hid_own[5:6, 0:POOL] = reorder(req_line).astype(BF16)
+    hid_own[6:7, 0:POOL] = reorder(idx_high).astype(BF16)
+    hid_own[7:8, 0:POOL] = reorder(idx_line - idx_high * 16.0).astype(BF16)
+    meta[1:2, 0:POOL] = req_line.astype(I32)
+    meta[1:2, POOL : 2 * POOL] = seen_line.astype(I32)
+    lane_w = lax.broadcasted_iota(I32, (1, WIDE), 1)
+    accepted_here = jnp.sum(
+        jnp.where(lane_w == w, small_len[1].astype(F32), 0.0), axis=1, keepdims=True
+    )
+    to_scalar = pltpu.make_async_copy(source_v, source, l_in.at[10])
+    to_scalar.start()
     hid_all[pl.ds(w, 1)] = hid_own[...][None]
-    meta_w[pl.ds(w, 1)] = meta[...][None]
     meta_n[pl.ds(n, 1)] = meta[...][None]
-    enter(w, n)
-
-    def send_hidden(k, _):
-        remote(hid_own, hid_all.at[w], s_a, r_a, ((w + k) % WIDE, n)).start()
-        return 0
-
-    lax.fori_loop(1, WIDE, send_hidden, 0)
-
-    def send_meta(k, _):
-        remote(meta, meta_w.at[w], s_m, r_m, ((w + k) % WIDE, n)).start()
-        return 0
-
-    def send_meta_narrow(k, _):
-        remote(meta, meta_n.at[n], s_mn, r_mn, (w, (n + k) % NARROW)).start()
-        return 0
-
-    lax.fori_loop(1, NARROW, send_meta_narrow, 0)
+    pl.semaphore_wait(barrier, WIDE + NARROW - 2)
 
     def block_of(part, head):
         return pl.ds(pl.multiple_of(KVH * HD * part + HD * head, HD), HD)
@@ -157,16 +178,24 @@
             (w, 2 * tx + c),
         ).start()
 
-    own_copies = []
+    for dx, part in EARLY:
+        exchange(dx, part)
+
+    def send_hidden(k, _):
+        remote(hid_own, hid_all.at[w], s_a, r_a, ((w + k) % WIDE, n)).start()
+        return 0
+
+    lax.fori_loop(1, WIDE, send_hidden, 0)
+
+    def send_meta_narrow(k, _):
+        remote(meta, meta_n.at[n], s_mn, r_mn, (w, (n + k) % NARROW)).start()
+        return 0
+
+    lax.fori_loop(1, NARROW, send_meta_narrow, 0)
+
     for part in range(2):
         mine_here = pool.at[:, :, block_of(part, x)]
-        remote(mine_here, kv.at[n, part], s_p, r_p.at[0], (w, other)).start()
-        copy = pltpu.make_async_copy(mine_here, kv.at[n, part], l_sem.at[1 + part])
-        copy.start()
-        own_copies.append(copy)
-    for dx, part in EARLY:
-        exchange(dx, part)
-
+        remote(mine_here, kv.at[n, part], s_p, r_p.at[0, part], (w, other)).start()
     row = lax.broadcasted_iota(I32, (rows, WIDE * 8), 0).astype(F32)
     col = lax.broadcasted_iota(I32, (rows, WIDE * 8), 1).astype(F32)
     req_of_row = jnp.floor((row + 0.5) * 0.2)
@@ -184,10 +213,13 @@
     peaks[...] = jnp.full(peaks.shape, NEG, F32)
     acc[...] = jnp.zeros_like(acc)
 
-    load_pool.wait()
+    to_scalar.wait()
+    loads[6].wait()
 
     def take_page(j, _):
-        leaving[j] = pool_v[source[j]]
+        leaving[j] = pool_v[jnp.clip(source[0, j], 0, POOL - 1)]
+        for part in range(2):
+            kv[n, part, j] = pool_v[j, :, block_of(part, x)]
         return 0
 
     lax.fori_loop(0, POOL, take_page, 0)
@@ -224,8 +256,10 @@
     all_hidden = remote(others, others, s_a, r_a, (w, n))
     all_hidden.wait_recv()
     padded = hid_all[...].reshape(WIDE * 8, hid_all.shape[2])
+    loads[7].wait()
+    loads[8].wait()
     packed = jnp.dot(pick[...], padded, preferred_element_type=F32).astype(BF16)
-    part_q[...] = jnp.dot(packed, w_query[...], preferred_element_type=F32)
+    part_q[...] = jnp.dot(packed, w_query[...], preferred_element_type=F32).astype(BF16)
     to_hub_q = remote(part_q, sum_q.at[n], s_b, r_b, (w, z))
     to_hub_kv = remote(part_kv, sum_kv.at[n], s_bk, r_bk, (w, z))
 
@@ -245,7 +279,6 @@
 
     for dx, part in LATE:
         exchange(dx, part)
-    lax.fori_loop(1, WIDE, send_meta, 0)
     send_pages(1, CUT1)
     mine = query.at[y]
     seven_q = sum_q.at[pl.ds(0, 7)]
@@ -255,7 +288,7 @@
     def _():
         sum_q[pl.ds(n, 1)] = part_q[...][None]
         remote(seven_q, seven_q, s_b, r_b, (w, n)).wait_recv()
-        query[pl.ds(y, 1)] = jnp.sum(sum_q[...], axis=0).astype(BF16)[None]
+        query[pl.ds(y, 1)] = jnp.sum(sum_q[...].astype(F32), axis=0).astype(BF16)[None]
 
         def send_query(k, _):
             peer = ((z + k) % NZ) * NY + y
@@ -276,27 +309,32 @@
         sum_kv[pl.ds(n, 1)] = part_kv[...][None]
         remote(seven_kv, seven_kv, s_bk, r_bk, (w, n)).wait_recv()
         kv_tiles[...] = jnp.sum(sum_kv[...], axis=0).astype(BF16).reshape(8, 8, HD)
-        kv_four[pl.ds(y, 1)] = kv_tiles[pl.ds(w % 8, 1)]
+        kv_four[pl.ds(y, 1)] = kv_tiles[...][None]
 
         def send_tile(k, _):
-            peer = (w + k) % WIDE
-            remote(kv_tiles.at[peer % 8], kv_four.at[y], s_k1, r_k1, (peer, n)).start()
+            peer = ((z + k) % NZ) * NY + y
+            remote(kv_tiles, kv_four.at[y], s_k1, r_k1, (peer, n)).start()
             return 0
 
-        lax.fori_loop(1, WIDE, send_tile, 0)
+        lax.fori_loop(1, NZ, send_tile, 0)
 
     send_pages(CUT1, CUT2)
 
-    def relay(dx):
-        arrived = 2 * ((x + 4 - dx) % 4) + c
-        for part in range(2):
-            here = kv.at[arrived, part]
-            remote(here, here, s_x, r_x.at[dx - 1, part], (w, n)).wait_recv()
-        here = kv.at[arrived]
-        remote(here, here, s_p, r_p.at[dx], (w, other)).start()
-
-    relay(1)
-    relay(3)
+    def relay(dx, part):
+        here = kv.at[2 * ((x + 4 - dx) % 4) + c, part]
+        remote(here, here, s_x, r_x.at[dx - 1, part], (w, n)).wait_recv()
+        remote(here, here, s_p, r_p.at[dx, part], (w, other)).start()
+
+    for dx, part in EARLY:
+        relay(dx, part)
+    mine_kv = kv_four.at[y]
+
+    @pl.when(n != z)
+    def _():
+        remote(mine_kv, mine_kv, s_k1, r_k1, (w, n)).wait_recv()
+
+    for dy in (1, 3, 2):
+        remote(mine_kv, mine_kv, s_k3, r_k3, (z * NY + (y + dy) % NY, n)).start()
     narrow_tiles = meta_n.at[pl.ds(0, NARROW - 1)]
     remote(narrow_tiles, narrow_tiles, s_mn, r_mn, (w, n)).wait()
     page_meta = meta_n[:, 1, :].astype(F32).astype(BF16)
@@ -322,13 +360,9 @@
     spread_query = remote(three, three, s_c3, r_c3, (w, n))
     spread_query.wait_recv()
 
-    for copy in own_copies:
-        copy.wait()
     for g, dx in enumerate(ORDER):
-        if dx == 2:
-            relay(2)
-        from_other = kv.at[2 * ((x + 4 - dx) % 4) + (1 - c)]
-        remote(from_other, from_other, s_p, r_p.at[dx], (w, n)).wait_recv()
+        from_other = kv.at[2 * ((x + 4 - dx) % 4) + (1 - c), 0]
+        remote(from_other, from_other, s_p, r_p.at[dx, 0], (w, n)).wait_recv()
 
         def score(j, _, g=g, dx=dx):
             s = 2 * ((x + 4 - dx) % 4) + j // per
@@ -351,9 +385,13 @@
 
         lax.fori_loop(0, 2 * per, score, 0)
 
+    for dx, part in LATE:
+        relay(dx, part)
     peak = jnp.max(peaks[...], axis=1, keepdims=True)
     ones = jnp.ones((width, HD), BF16)
     for g, dx in enumerate(ORDER):
+        from_other = kv.at[2 * ((x + 4 - dx) % 4) + (1 - c), 1]
+        remote(from_other, from_other, s_p, r_p.at[dx, 1], (w, n)).wait_recv()
 
         def weigh(j, _, g=g, dx=dx):
             s = 2 * ((x + 4 - dx) % 4) + j // per
@@ -389,21 +427,12 @@
     received[pl.ds(w, 1)] = partial[pl.ds(w, 1)]
     send_pages(CUT2, CUT3)
 
-    four_tiles = kv_four
-    three_tiles = kv_four.at[pl.ds(0, 3)]
-
-    @pl.when(n != z)
-    def _():
-        remote(four_tiles, four_tiles, s_k1, r_k1, (w, n)).wait_recv()
-
-    @pl.when(n == z)
-    def _():
-        remote(three_tiles, three_tiles, s_k1, r_k1, (w, n)).wait_recv()
-
     lane = lax.broadcasted_iota(I32, (8, HD), 1)
+    three_kv = kv_four.at[pl.ds(0, 3)]
+    remote(three_kv, three_kv, s_k3, r_k3, (w, n)).wait()
     merged = jnp.zeros((8, HD), F32)
     for t in range(4):
-        turned = pltpu.roll(kv_four[t].astype(F32), (t + 4 - w // 8) % 4 * 32, 1)
+        turned = pltpu.roll(kv_four[t, w % 8].astype(F32), (t + 4 - w // 8) % 4 * 32, 1)
         merged = merged + jnp.where((lane >= 32 * t) & (lane < 32 * t + 32), turned, 0.0)
     kv_new[pl.ds(n, 1)] = merged.astype(BF16)[None]
 
@@ -412,25 +441,30 @@
         return 0
 
     lax.fori_loop(1, NARROW, send_new, 0)
-    wide_tiles = meta_w.at[pl.ds(0, WIDE - 1)]
-    remote(wide_tiles, wide_tiles, s_m, r_m, (w, n)).wait()
-    to_scalar = pltpu.make_async_copy(meta_w.at[:, 0], meta_s, l_sem.at[4])
-    to_scalar.start()
-    to_scalar.wait()
-
-    def moved_meta(i, _):
+    meta_lane = lax.broadcasted_iota(I32, (WIDE, HD), 1)
+    slot_source = lax.broadcasted_iota(I32, (WIDE, POOL), 0)
+    slot_lane = lax.broadcasted_iota(I32, (WIDE, POOL), 1)
+
+    def arrived(line):
+        values = hid_all[:, line : line + 1, 0:HD].astype(F32).reshape(WIDE, HD)
+        result = jnp.zeros((1, POOL), F32)
         for k in range(2):
-            moved_req[2 * i + k] = meta_s[i, 2 * w + k]
-            moved_idx[2 * i + k] = meta_s[i, POOL + 2 * w + k]
-        return 0
-
-    lax.fori_loop(0, WIDE, moved_meta, 0)
+            column = jnp.sum(
+                jnp.where(meta_lane == 2 * w + k, values, 0.0), axis=1, keepdims=True
+            )
+            result = result + jnp.sum(
+                jnp.where(slot_lane == 2 * slot_source + k, column, 0.0), axis=0, keepdims=True
+            )
+        return result
+
+    moved_req[...] = arrived(5).astype(I32)
+    moved_idx[...] = (arrived(6) * 16.0 + arrived(7)).astype(I32)
     seven_new = kv_new.at[pl.ds(0, 7)]
     remote(seven_new, seven_new, s_k2, r_k2, (w, n)).wait()
-    step = lax.broadcasted_iota(I32, (STEPS, HD), 0)
+    step = lax.broadcasted_iota(I32, (STEPS, HD), 0).astype(F32)
     for b in range(8):
         entries[0, :, HD * b : HD * b + HD] = jnp.where(
-            step < accepted[w], kv_new[b][0:STEPS, :].astype(F32), 0.0
+            step < accepted_here, kv_new[b][0:STEPS, :].astype(F32), 0.0
         ).astype(BF16)
 
     first_row = lax.broadcasted_iota(I32, (32, rows), 0)
@@ -498,6 +532,7 @@
     others = gathered.at[pl.ds(0, WIDE - 1)]
     all_rows = remote(others, others, s_g, r_g, (w, n))
     all_rows.wait_recv()
+    loads[9].wait()
     attn = gathered[...].reshape(WIDE * 8, gathered.shape[2])
     product = jnp.dot(attn, w_out[...], preferred_element_type=F32)
     send_e[...] = product.astype(BF16).reshape(NARROW, 32, HD)
@@ -521,18 +556,19 @@
     three = kv.at[pl.ds(0, 3)]
     remote(three, three, s_x, r_x.at[0, 0], (w, n)).wait_send()
     four = kv.at[pl.ds(0, 4)]
-    remote(four, four, s_p, r_p.at[0], (w, n)).wait_send()
+    remote(four, four, s_p, r_p.at[0, 0], (w, n)).wait_send()
 
     @pl.when(n != z)
     def _():
         to_hub_q.wait_send()
         to_hub_kv.wait_send()
 
-    tiles31 = received.at[pl.ds(0, 31), 0]
+    three_kv = kv_four.at[pl.ds(0, 3)]
 
     @pl.when(n == z)
     def _():
-        remote(tiles31, tiles31, s_k1, r_k1, (w, n)).wait_send()
+        remote(kv_four, kv_four, s_k1, r_k1, (w, n)).wait_send()
+        remote(three_kv, three_kv, s_k1, r_k1, (w, n)).wait_send()
         four_q = query
         three_q = query.at[pl.ds(0, 3)]
         remote(four_q, four_q, s_c2, r_c2, (w, n)).wait_send()
@@ -546,47 +582,71 @@
     remote(gone, gone, s_mig, r_mig, (w, n)).wait()
 
 
+def deliver_kernel(*refs):
+    sources, targets, (pages, sem_in, sem_out, sem_small) = refs[0:5], refs[5:10], refs[10:14]
+    size = POOL // PIECES
+    small = [
+        pltpu.make_async_copy(sources[i], targets[i], sem_small.at[i]) for i in (0, 1, 3, 4)
+    ]
+    for copy in small:
+        copy.start()
+    parts = [pl.ds(size * i, size) for i in range(PIECES)]
+    coming = [
+        pltpu.make_async_copy(sources[2].at[part], pages.at[part], sem_in.at[i])
+        for i, part in enumerate(parts)
+    ]
+    going = [
+        pltpu.make_async_copy(pages.at[part], targets[2].at[part], sem_out.at[i])
+        for i, part in enumerate(parts)
+    ]
+    for copy in coming:
+        copy.start()
+    for before, after in zip(coming, going):
+        before.wait()
+        after.start()
+    for copy in going + small:
+        copy.wait()
+
+
 def on_device(hidden, w_query, w_keyval, w_out, pool, page_req, page_idx, lengths, moves, accepted):
     dma = pltpu.SemaphoreType.DMA
     shape = jax.ShapeDtypeStruct
-    source, meta = pl.pallas_call(
-        order_kernel,
-        out_shape=(shape((POOL,), I32), shape((8, 128), I32)),
-        in_specs=[SMEM_SPEC] * 4,
-        out_specs=(SMEM_SPEC, SMEM_SPEC),
-        scratch_shapes=[pltpu.SMEM((WIDE,), I32)],
-        name="order_pages",
-    )(moves.reshape(POOL), page_req, page_idx, lengths)
-
     depth = hidden.shape[1]
     rows = WIDE * STEPS
     width = CHUNK * PAGE
     chunks = NARROW * POOL // CHUNK
-    attended, entries, moved, moved_req, moved_idx = pl.pallas_call(
+    results = pl.pallas_call(
         whole_kernel,
         out_shape=(
             shape((4 * STEPS, HD), BF16),
             shape((1, STEPS, 1024), BF16),
             shape(pool.shape, BF16),
-            shape((POOL,), I32),
-            shape((POOL,), I32),
+            shape((1, POOL), I32),
+            shape((1, POOL), I32),
         ),
-        in_specs=[SMEM_SPEC] * 2 + [VMEM_SPEC] * 5 + [ANY_SPEC],
-        out_specs=(VMEM_SPEC, VMEM_SPEC, ANY_SPEC, SMEM_SPEC, SMEM_SPEC),
+        in_specs=[ANY_SPEC] * 10,
+        out_specs=(VMEM_SPEC, VMEM_SPEC, ANY_SPEC, VMEM_SPEC, VMEM_SPEC),
         scratch_shapes=[
+            pltpu.VMEM((3, 1, POOL), I32),
+            pltpu.VMEM((2, 1, WIDE), I32),
+            pltpu.VMEM((STEPS, depth), BF16),
+            pltpu.VMEM(w_query.shape, BF16),
+            pltpu.VMEM(w_keyval.shape[::-1], BF16),
+            pltpu.VMEM(w_out.shape, BF16),
+            pltpu.VMEM((8, 128), I32),
+            pltpu.VMEM((8, 128), I32),
+            pltpu.SMEM((8, 128), I32),
             pltpu.VMEM((8, depth), BF16),
             pltpu.VMEM((WIDE, 8, depth), BF16),
-            pltpu.VMEM((rows, HD), F32),
+            pltpu.VMEM((rows, HD), BF16),
             pltpu.VMEM((64, HD), F32),
-            pltpu.VMEM((NARROW, rows, HD), F32),
+            pltpu.VMEM((NARROW, rows, HD), BF16),
             pltpu.VMEM((NARROW, 64, HD), F32),
             pltpu.VMEM((4, rows, HD), BF16),
             pltpu.VMEM((8, 8, HD), BF16),
-            pltpu.VMEM((4, 8, HD), BF16),
+            pltpu.VMEM((4, 8, 8, HD), BF16),
             pltpu.VMEM((8, 8, HD), BF16),
-            pltpu.VMEM((WIDE, 8, 128), I32),
             pltpu.VMEM((NARROW, 8, 128), I32),
-            pltpu.SMEM((WIDE, 128), I32),
             pltpu.VMEM(pool.shape, BF16),
             pltpu.VMEM(pool.shape, BF16),
             pltpu.VMEM((NARROW, 2, POOL, PAGE, HD), BF16),
@@ -602,17 +662,41 @@
             pltpu.VMEM((WIDE, 8, 4 * HD), BF16),
             pltpu.VMEM((NARROW, 32, HD), BF16),
             pltpu.VMEM((NARROW, 32, HD), BF16),
+            dma((11,)), dma, dma, dma, dma, dma, dma,
+            dma((5,)), dma, dma((3, 2)), dma, dma((4, 2)),
+            dma, dma, dma, dma, dma, dma, dma, dma, dma, dma, dma, dma,
             dma, dma, dma, dma, dma, dma, dma, dma,
-            dma((5,)), dma, dma((3, 2)), dma, dma((4,)),
-            dma, dma, dma, dma, dma, dma, dma, dma, dma, dma, dma, dma,
-            dma, dma, dma, dma, dma, dma,
         ],
         compiler_params=pltpu.CompilerParams(
-            collective_id=0, has_side_effects=True, vmem_limit_bytes=50 << 20
+            collective_id=0, has_side_effects=True, vmem_limit_bytes=60 << 20
         ),
         name="verify_step",
-    )(source, accepted, hidden, w_query, w_keyval.T, w_out, meta, pool)
-    return attended, entries, moved, moved_req, moved_idx
+    )(
+        moves.reshape(1, POOL),
+        page_req.reshape(1, POOL),
+        page_idx.reshape(1, POOL),
+        lengths.reshape(1, WIDE),
+        accepted.reshape(1, WIDE),
+        hidden,
+        w_query,
+        w_keyval.T,
+        w_out,
+        pool,
+    )
+    attended, entries, moved, moved_req, moved_idx = pl.pallas_call(
+        deliver_kernel,
+        out_shape=[shape(r.shape, r.dtype) for r in results],
+        in_specs=[ANY_SPEC] * 5,
+        out_specs=[ANY_SPEC] * 5,
+        scratch_shapes=[
+            pltpu.VMEM(pool.shape, BF16),
+            dma((PIECES,)),
+            dma((PIECES,)),
+            dma((5,)),
+        ],
+        name="deliver",
+    )(*results)
+    return attended, entries, moved, moved_req.reshape(POOL), moved_idx.reshape(POOL)
 
 
 def solution(mesh):

time: 119 us -> 100 us (0.84)
  the two profiles are of different devices: /device:TPU:1 before, /device:TPU:70 now
where the time goes in v4:
time: 100 us
  Pallas kernels  99.5 us (100%)
    pallas_call x1, Pallas kernels, on_device(): pl.pallas_call(whole_kernel, out_shape=(shape((4 * STEPS, HD), BF16), sha...  97 us
    pallas_call x1, Pallas kernels, on_device(): pl.pallas_call(deliver_kernel, out_shape=[shape(r.shape, r.dtype) for r i...  2.48 us

profile of v4, /device:TPU:70, one launch (start us, length us, event | category | flops | bytes accessed | tf_op | source)
XLA Modules:
  0.0 100.1 jit_solution(10092336827514832251)
XLA Ops:
  0.6 97.0 %verify_step.1 = (bf16[20,128]{1,0:T(8,128)(2,1)}, bf16[1,5,1024]{2,1,0:T(8,128)(2,1)}, bf16[64,16,1024]{2,1,0:T(8,128)(2,1)}, s32[1,64]{1,0:T(1,128)}, s32[1,64]{1,0:T(1,128)}) custom-call(s32[1,64]{1,0:T(1,128)} %bitcast.9, s32[1,64]{1,0:T(1,128)} %bitcast.10, s32[1,64]{1,0:T(1,128)} %bitcast.11, s32[1,32]{1,0:T(1,128)} %bitcast.12, s32[1,32]{1,0:T(1,128)} %bitcast.13, ...), custom_call_target="tpu_custom_call" | custom-call | tf_op jit(solution)/shard_map/verify_step/pallas_call | solution.py:618
  97.6 2.5 %deliver.1 = (bf16[20,128]{1,0:T(8,128)(2,1)}, bf16[1,5,1024]{2,1,0:T(8,128)(2,1)}, bf16[64,16,1024]{2,1,0:T(8,128)(2,1)}, s32[1,64]{1,0:T(1,128)}, s32[1,64]{1,0:T(1,128)}) custom-call(bf16[20,128]{1,0:T(8,128)(2,1)} %get-tuple-element.15.refs_0_, bf16[1,5,1024]{2,1,0:T(8,128)(2,1)} %get-tuple-element.16.refs_1_, ...), custom_call_target="tpu_custom_call" | custom-call | tf_op jit(solution)/shard_map/deliver/pallas_call | solution.py:686

commit v5 on v4

--- a/solution.py
+++ b/solution.py
@@ -20,12 +20,13 @@
 POOL = 64
 CHUNK = 32
 PIECES = 4
-EARLY = ((2, 0), (1, 0), (3, 0))
-LATE = ((2, 1), (1, 1), (3, 1))
+EARLY = ((2, 0), (1, 0), (3, 0), (2, 1))
+LATE = ((1, 1), (3, 1))
 ORDER = (0, 2, 1, 3)
+CUT0 = 6
 CUT1 = 8
 CUT2 = 14
-CUT3 = 14
+CUT3 = 15
 SCALE = 1.0 / math.sqrt(HD)
 LOG2E = 1.4426950408889634
 NEG = -1e30
@@ -252,6 +253,7 @@
                 (peer, n),
             ).start()
 
+    send_pages(1, CUT0)
     others = hid_all.at[pl.ds(0, WIDE - 1)]
     all_hidden = remote(others, others, s_a, r_a, (w, n))
     all_hidden.wait_recv()
@@ -279,7 +281,7 @@
 
     for dx, part in LATE:
         exchange(dx, part)
-    send_pages(1, CUT1)
+    send_pages(CUT0, CUT1)
     mine = query.at[y]
     seven_q = sum_q.at[pl.ds(0, 7)]
     seven_kv = sum_kv.at[pl.ds(0, 7)]

time: 100 us -> 96.8 us (0.968)
  the two profiles are of different devices: /device:TPU:70 before, /device:TPU:1 now
where the time goes in v5:
time: 96.8 us; the launch traced here: 96.7 us
  Pallas kernels  96 us (99%)
    pallas_call x1, Pallas kernels, on_device(): pl.pallas_call(whole_kernel, out_shape=(shape((4 * STEPS, HD), BF16), sha...  93.5 us
    pallas_call x1, Pallas kernels, on_device(): pl.pallas_call(deliver_kernel, out_shape=[shape(r.shape, r.dtype) for r i...  2.48 us

profile of v5, /device:TPU:1, one launch (start us, length us, event | category | flops | bytes accessed | tf_op | source)
XLA Modules:
  0.0 96.7 jit_solution(4670093095901941000)
XLA Ops:
  0.6 93.5 %verify_step.1 = (bf16[20,128]{1,0:T(8,128)(2,1)}, bf16[1,5,1024]{2,1,0:T(8,128)(2,1)}, bf16[64,16,1024]{2,1,0:T(8,128)(2,1)}, s32[1,64]{1,0:T(1,128)}, s32[1,64]{1,0:T(1,128)}) custom-call(s32[1,64]{1,0:T(1,128)} %bitcast.9, s32[1,64]{1,0:T(1,128)} %bitcast.10, s32[1,64]{1,0:T(1,128)} %bitcast.11, s32[1,32]{1,0:T(1,128)} %bitcast.12, s32[1,32]{1,0:T(1,128)} %bitcast.13, ...), custom_call_target="tpu_custom_call" | custom-call | tf_op jit(solution)/shard_map/verify_step/pallas_call | solution.py:620
  94.2 2.5 %deliver.1 = (bf16[20,128]{1,0:T(8,128)(2,1)}, bf16[1,5,1024]{2,1,0:T(8,128)(2,1)}, bf16[64,16,1024]{2,1,0:T(8,128)(2,1)}, s32[1,64]{1,0:T(1,128)}, s32[1,64]{1,0:T(1,128)}) custom-call(bf16[20,128]{1,0:T(8,128)(2,1)} %get-tuple-element.15.refs_0_, bf16[1,5,1024]{2,1,0:T(8,128)(2,1)} %get-tuple-element.16.refs_1_, ...), custom_call_target="tpu_custom_call" | custom-call | tf_op jit(solution)/shard_map/deliver/pallas_call | solution.py:688

commit v6 on v5

--- a/solution.py
+++ b/solution.py
@@ -273,7 +273,7 @@
         padded, w_kv_t[...], (((1,), (1,)), ((), ())), preferred_element_type=F32
     )
     for j in range(4):
-        part_kv[:, 32 * j : 32 * j + 32] = new_kv[64 * j : 64 * j + 64]
+        part_kv[:, 32 * j : 32 * j + 32] = new_kv[64 * j : 64 * j + 64].astype(BF16)
 
     @pl.when(n != z)
     def _():
@@ -310,7 +310,7 @@
     def _():
         sum_kv[pl.ds(n, 1)] = part_kv[...][None]
         remote(seven_kv, seven_kv, s_bk, r_bk, (w, n)).wait_recv()
-        kv_tiles[...] = jnp.sum(sum_kv[...], axis=0).astype(BF16).reshape(8, 8, HD)
+        kv_tiles[...] = jnp.sum(sum_kv[...].astype(F32), axis=0).astype(BF16).reshape(8, 8, HD)
         kv_four[pl.ds(y, 1)] = kv_tiles[...][None]
 
         def send_tile(k, _):
@@ -641,9 +641,9 @@
             pltpu.VMEM((8, depth), BF16),
             pltpu.VMEM((WIDE, 8, depth), BF16),
             pltpu.VMEM((rows, HD), BF16),
-            pltpu.VMEM((64, HD), F32),
+            pltpu.VMEM((64, HD), BF16),
             pltpu.VMEM((NARROW, rows, HD), BF16),
-            pltpu.VMEM((NARROW, 64, HD), F32),
+            pltpu.VMEM((NARROW, 64, HD), BF16),
             pltpu.VMEM((4, rows, HD), BF16),
             pltpu.VMEM((8, 8, HD), BF16),
             pltpu.VMEM((4, 8, 8, HD), BF16),

time: 96.8 us -> 96.7 us (level)
  no operation moved by 1% of the time
where the time goes in v6:
time: 96.7 us; the launch traced here: 96.6 us
  Pallas kernels  96 us (99%)
    pallas_call x1, Pallas kernels, on_device(): pl.pallas_call(whole_kernel, out_shape=(shape((4 * STEPS, HD), BF16), sha...  93.5 us
    pallas_call x1, Pallas kernels, on_device(): pl.pallas_call(deliver_kernel, out_shape=[shape(r.shape, r.dtype) for r i...  2.48 us

profile of v6, /device:TPU:1, one launch (start us, length us, event | category | flops | bytes accessed | tf_op | source)
XLA Modules:
  0.0 96.6 jit_solution(5198793346910262667)
XLA Ops:
  0.6 93.5 %verify_step.1 = (bf16[20,128]{1,0:T(8,128)(2,1)}, bf16[1,5,1024]{2,1,0:T(8,128)(2,1)}, bf16[64,16,1024]{2,1,0:T(8,128)(2,1)}, s32[1,64]{1,0:T(1,128)}, s32[1,64]{1,0:T(1,128)}) custom-call(s32[1,64]{1,0:T(1,128)} %bitcast.9, s32[1,64]{1,0:T(1,128)} %bitcast.10, s32[1,64]{1,0:T(1,128)} %bitcast.11, s32[1,32]{1,0:T(1,128)} %bitcast.12, s32[1,32]{1,0:T(1,128)} %bitcast.13, ...), custom_call_target="tpu_custom_call" | custom-call | tf_op jit(solution)/shard_map/verify_step/pallas_call | solution.py:620
  94.1 2.5 %deliver.1 = (bf16[20,128]{1,0:T(8,128)(2,1)}, bf16[1,5,1024]{2,1,0:T(8,128)(2,1)}, bf16[64,16,1024]{2,1,0:T(8,128)(2,1)}, s32[1,64]{1,0:T(1,128)}, s32[1,64]{1,0:T(1,128)}) custom-call(bf16[20,128]{1,0:T(8,128)(2,1)} %get-tuple-element.15.refs_0_, bf16[1,5,1024]{2,1,0:T(8,128)(2,1)} %get-tuple-element.16.refs_1_, ...), custom_call_target="tpu_custom_call" | custom-call | tf_op jit(solution)/shard_map/deliver/pallas_call | solution.py:688
